TPU v7x, 32 devices: a whole 2x2x4 slice. The times are simulated.
32 devices in a mesh: cube: 4 (over z), row: 2 (over y), col: 4 (over x, core).
Axes of the slice: x: 2, y: 2, z: 4, core: 2. Of those that a mesh axis runs over, the one named last changes fastest.
Arguments:
- diag_block: float32 [4, 512, 512], P('cube', ('row', 'col')), may hold values from -1 to 4, as said below
- panel: float32 [4, 16384, 512], P('cube', 'row', 'col'), may hold values from -2 to 2
- pattern: int32 [4, 128, 4], P('cube', 'row', 'col'), may hold values 0 or 1
- contribution: float32 [4, 16384, 512], P('cube', 'row', 'col'), may hold values from -6 to 6
- route: int32 [4, 128, 1], P('cube', 'row'), may hold values from 0 to 3; in each aligned block of 64 rows (0 to 63, 64 to 127, ..., all dimensions but the last counted through in order) at most 32 rows name the same one
- slot: int32 [4, 128], P('cube', 'row'), may hold values from 0 to 31
Outputs:
- diag_factor: float32 [4, 512, 512], P('cube', ('row', 'col'))
- panel_factor: float32 [4, 16384, 512], P('cube', 'row', 'col')
- assembled: float32 [4, 8192, 512], P('cube', 'row', 'col')
Inputs may be any that keep to these rules, and one draw needn't show every extreme that they name: `diag_block`: each 512 x 512 block is symmetric with positive diagonal larger than the sum of magnitudes of the rest of its row. `route`: within the 64 rows of one device, no value names more than 32 blocks.
All inputs are finite; a program needn't handle non-finite values. No bound on the sum of `pattern` on one device may be relied on, other than what follows from the above.
Results may differ from a plain program's by a relative error of at most 0.0001.
Values sent between devices are 32-bit elements; how exact they have to be, the bound alone decides.
A program may use at most 128 MiB of HBM per device.

v0:
```python
import functools

import jax
import jax.numpy as jnp
from jax import lax
from jax.experimental import pallas as pl
from jax.experimental.pallas import tpu as pltpu
from jax.sharding import PartitionSpec as P

BS = 128
HIGHEST = lax.Precision.HIGHEST
NT = (((1,), (1,)), ((), ()))
ANY = pl.BlockSpec(memory_space=pl.ANY)
VMEM = pl.BlockSpec(memory_space=pltpu.VMEM)
SMEM = pl.BlockSpec(memory_space=pltpu.SMEM)
MESH = pl.DeviceIdType.MESH


def remote(src, dst, send, recv, device):
    return pltpu.make_async_remote_copy(
        src_ref=src, dst_ref=dst, send_sem=send, recv_sem=recv,
        device_id=device, device_id_type=MESH,
    )


def factor_block(s_ref, x_ref):
    n = BS
    sub = lax.broadcasted_iota(jnp.int32, (n, n), 0)
    lane = lax.broadcasted_iota(jnp.int32, (n, n), 1)
    x_ref[...] = (sub == lane).astype(jnp.float32)
    step = 32
    for lo in range(0, n, step):
        rows = n - lo
        lane_r = lax.broadcasted_iota(jnp.int32, (rows, n), 1)
        sub_c = lax.broadcasted_iota(jnp.int32, (rows, 1), 0) + lo
        lane_1 = lax.broadcasted_iota(jnp.int32, (1, n), 1)

        def body(j, carry):
            s = s_ref[pl.ds(lo, rows), :]
            x = x_ref[pl.ds(lo, rows), :]
            row_s = s_ref[pl.ds(j, 1), :]
            row_x = x_ref[pl.ds(j, 1), :]
            col = jnp.sum(jnp.where(lane_r == j, s, 0.0), axis=1, keepdims=True)
            pivot = jnp.sum(jnp.where(lane_1 == j, row_s, 0.0), axis=1, keepdims=True)
            scale = 1.0 / pivot
            col = jnp.where(sub_c > j, col, 0.0)
            s_ref[pl.ds(lo, rows), :] = s - col * (row_s * scale)
            x_ref[pl.ds(lo, rows), :] = x - col * (row_x * scale)
            return carry

        lax.fori_loop(lo, lo + step, body, 0)


def cholesky_inverse(a_ref, inv_ref, s_ref, x_ref, between):
    width = a_ref.shape[0]
    sub = lax.broadcasted_iota(jnp.int32, (BS, BS), 0)
    lane = lax.broadcasted_iota(jnp.int32, (BS, BS), 1)
    inv_ref[...] = jnp.zeros_like(inv_ref)
    for p in range(width // BS):
        o, e = p * BS, (p + 1) * BS
        s_ref[...] = a_ref[o:e, o:e]
        factor_block(s_ref, x_ref)
        s = s_ref[...]
        d = jnp.sum(jnp.where(lane == sub, s, 0.0), axis=1, keepdims=True)
        rs = 1.0 / jnp.sqrt(d)
        low = jnp.transpose(jnp.where(lane >= sub, s, 0.0) * rs)
        x = x_ref[...] * rs
        a_ref[o:e, o:e] = low
        inv_ref[o:e, o:e] = x
        if e < width:
            below = lax.dot_general(a_ref[e:, o:e], x, NT, precision=HIGHEST)
            a_ref[e:, o:e] = below
            a_ref[e:, e:] = a_ref[e:, e:] - lax.dot_general(below, below, NT, precision=HIGHEST)
            a_ref[o:e, e:] = jnp.zeros((BS, width - e), jnp.float32)
        if p > 0:
            part = jnp.dot(a_ref[o:e, :o], inv_ref[:o, :o], precision=HIGHEST)
            inv_ref[o:e, :o] = -jnp.dot(x, part, precision=HIGHEST)
        between(p)


def gather_kernel(chunks, prev_ref, prev_on, last_ref, last_on, diag_ref, mask_ref, panel_ref, contribution_ref, f_ref, out_ref, l_ref,
                  own, g0, g1, g2, contrib, a_ref, inv_ref, s_ref, x_ref, h_ref, hc_ref, w_ref,
                  vh_ref, vl_ref, masks, head_masks, fs, t_ref, ra, rb, ra2, rb2,
                  dsend, drecv, xsend, xrecv, fsend, frecv, psend, precv, hsend, hrecv,
                  msend, mrecv, lsem, isem, osem,
                  asend, arecv, bsend, brecv, a2send, a2recv, b2send, b2recv):
    z = lax.axis_index("cube")
    m = z % 2
    r, c = lax.axis_index("row"), lax.axis_index("col")
    y = 1 - r
    c1 = c + 1 - 2 * (c % 2)
    c2 = (c + 2) % 4
    c3 = (c1 + 2) % 4
    order = (c, c1, c2, c3)
    pieces = (own, g0, g1, g2)
    ndiag = diag_ref.shape[0]
    rows = panel_ref.shape[0] // chunks
    to_x, to_core, to_row = {"col": c2}, {"col": c1}, {"row": y}

    load_own = pltpu.make_async_copy(panel_ref, own, isem.at[0])
    load_contrib = pltpu.make_async_copy(contribution_ref, contrib, isem.at[1])
    barrier = pltpu.get_barrier_semaphore()
    to_cube = {"cube": z + 1 - 2 * m}
    for device in (to_x, to_core, to_row, to_cube):
        pl.semaphore_signal(barrier, inc=1, device_id=device, device_id_type=MESH)
    pl.semaphore_wait(barrier, 4)

    def spot(rr, cc):
        return a_ref.at[pl.ds(pl.multiple_of((rr * 4 + cc) * ndiag, ndiag), ndiag)]

    def diag_copy(k, src, rr, cc, device):
        return remote(src, spot(rr, cc), dsend.at[k], drecv.at[k], device)

    def across(i):
        part = pl.ds(pl.multiple_of(i * rows, rows), rows)
        return remote(panel_ref.at[part], g1.at[part], xsend.at[i], xrecv.at[i], to_x)

    def onward(i):
        part = pl.ds(pl.multiple_of(i * rows, rows), rows)
        return remote(g1.at[part], g2.at[part], fsend.at[i], frecv.at[i], to_core)

    own_piece = remote(panel_ref, g0, psend, precv, to_core)
    mask_x = remote(mask_ref, masks.at[2], msend.at[0], mrecv.at[0], to_x)
    mask_core = remote(mask_ref, masks.at[1], msend.at[1], mrecv.at[1], to_core)
    mask_on = remote(masks.at[2], masks.at[3], msend.at[2], mrecv.at[2], to_core)

    first = diag_copy(0, diag_ref, r, c, to_x)
    first.start()
    mask_x.start()
    for i in range(chunks):
        across(i).start()
    second = [diag_copy(1, diag_ref, r, c, to_row)]
    second[0].start()
    mask_core.start()
    load_own.start()
    load_contrib.start()
    a_ref[pl.ds(pl.multiple_of((r * 4 + c) * ndiag, ndiag), ndiag), :] = diag_ref[...]
    masks[0] = mask_ref[...]
    first.wait_recv()
    second.append(diag_copy(2, spot(r, c2), r, c2, to_row))
    second[1].start()
    third = [
        diag_copy(3, diag_ref, r, c, to_core),
        diag_copy(4, spot(r, c2), r, c2, to_core),
    ]
    for copy in third:
        copy.start()
    mask_x.wait_recv()
    mask_on.start()
    for copy in second:
        copy.wait_recv()
    third.append(diag_copy(5, spot(y, c), y, c, to_core))
    third.append(diag_copy(6, spot(y, c2), y, c2, to_core))
    for copy in third[2:]:
        copy.start()
    for copy in third:
        copy.wait_recv()
    for copy in [first] + second + third:
        copy.wait_send()
    own_piece.start()

    ahead = chunks // 2

    def between(p):
        for i in range(p * ahead // 4, (p + 1) * ahead // 4):
            across(i).wait_recv()
            onward(i).start()

    cholesky_inverse(a_ref, inv_ref, s_ref, x_ref, between)
    l_ref[...] = a_ref[pl.ds(pl.multiple_of((r * 4 + c) * ndiag, ndiag), ndiag), :]

    load_own.wait()
    load_contrib.wait()
    own_piece.wait_recv()
    mask_core.wait_recv()
    mask_on.wait_recv()
    early = max(1, 4 * BS // rows)
    for i in range(early):
        onward(i).wait_recv()
    head = remote(h_ref, h_ref, hsend.at[0], hrecv.at[0], to_row)
    head_mask = remote(masks, head_masks, hsend.at[1], hrecv.at[1], to_row)
    window = pl.ds(pl.multiple_of(c * BS, BS), BS)

    @pl.when(r == 0)
    def _():
        loads = [
            pltpu.make_async_copy(piece.at[window], h_ref.at[j], lsem.at[j])
            for j, piece in enumerate(pieces)
        ]
        for copy in loads:
            copy.start()
        for copy in loads:
            copy.wait()
        head.start()
        head_mask.start()
        for j, k in enumerate(order):
            hc_ref[:, pl.ds(pl.multiple_of(k * BS, BS), BS)] = h_ref[j] * masks[j, pl.ds(c, 1), :]
        head.wait_send()
        head_mask.wait_send()

    @pl.when(r == 1)
    def _():
        head.wait_recv()
        head_mask.wait_recv()
        for j, k in enumerate(order):
            hc_ref[:, pl.ds(pl.multiple_of(k * BS, BS), BS)] = h_ref[j] * head_masks[j, pl.ds(c, 1), :]

    factor_head = lax.dot_general(hc_ref[...], inv_ref[...], NT, precision=HIGHEST)
    w_ref[pl.ds(BS, BS), :] = jnp.dot(factor_head, inv_ref[...], precision=HIGHEST)
    w_ref[pl.ds(0, BS), :] = inv_ref[pl.ds(pl.multiple_of(c * BS, BS), BS), :]
    for j, k in enumerate(order):
        high, low = split(jnp.transpose(w_ref[:, pl.ds(pl.multiple_of(k * BS, BS), BS)]))
        vh_ref[j * BS:(j + 1) * BS, :] = high
        vl_ref[j * BS:(j + 1) * BS, :] = low

    def stores(i, buf):
        part = pl.ds(pl.multiple_of(i * rows, rows), rows)
        return (pltpu.make_async_copy(fs.at[buf], f_ref.at[part], osem.at[buf]),)

    def compute(i):
        buf = i % 2

        @pl.when(i >= 2)
        def _():
            for copy in stores(i - 2, buf):
                copy.wait()

        start = pl.multiple_of(i * rows, rows)
        blocks = []
        for b in range(rows // BS):
            part = pl.ds(pl.multiple_of(start + b * BS, BS), BS)
            at = i * (rows // BS) + b
            blocks.append(jnp.concatenate(
                [piece[part, :] * masks[j, pl.ds(at, 1), :] for j, piece in enumerate(pieces)], axis=1))
        high, low = split(jnp.concatenate(blocks, axis=0))
        dot = functools.partial(jnp.dot, preferred_element_type=jnp.float32)
        out = dot(high, vh_ref[...]) + (dot(high, vl_ref[...]) + dot(low, vh_ref[...]))
        fs[buf] = out[:, :BS]
        for copy in stores(i, buf):
            copy.start()
        for b in range(rows // BS):
            at = i * (rows // BS) + b
            update = contrib[at] - out[b * BS:(b + 1) * BS, BS:]
            contrib[at] = update + prev_on[at] * contrib[prev_ref[at]]

    def step(i, carry):
        @pl.when((i >= ahead) & (i < chunks))
        def _():
            across(i).wait_recv()
            onward(i).start()

        @pl.when(i > early)
        def _():
            onward(i - 1).wait_recv()

        @pl.when(i > 0)
        def _():
            compute(i - 1)
        return carry

    lax.fori_loop(0, chunks + 1, step, 0)
    slots = out_ref.shape[0]

    def fill(h, rr, begin, end):
        def body(k, carry):
            name = (h * 2 + rr) * slots + k
            t_ref[h * 2 + rr, k] = contrib[last_ref[name]] * last_on[name]
            return carry

        lax.fori_loop(begin, end, body, 0)

    route_slots(m, r, y, to_row, to_cube, fill, t_ref, out_ref, ra, rb, ra2, rb2,
                asend, arecv, bsend, brecv, a2send, a2recv, b2send, b2recv)
    for i in (chunks - 2, chunks - 1):
        for copy in stores(i, i % 2):
            copy.wait()
    for i in range(chunks):
        across(i).wait_send()
        onward(i).wait_send()
    own_piece.wait_send()
    for copy in (mask_x, mask_core, mask_on):
        copy.wait_send()


def factor_and_route(chains, diag, mask, panel, contribution, pblk):
    chunks = 16
    rows, share = panel.shape
    tile = rows // chunks
    half = pblk // 2
    parts = half // 4
    ndiag, width = diag.shape
    piece = jax.ShapeDtypeStruct((rows, share), jnp.float32)
    whole = pltpu.VMEM((rows, share), jnp.float32)
    square = pltpu.VMEM((width, width), jnp.float32)
    block = pltpu.VMEM((BS, BS), jnp.float32)
    sems = pltpu.SemaphoreType.DMA
    return pl.pallas_call(
        functools.partial(gather_kernel, chunks),
        out_shape=(
            piece,
            jax.ShapeDtypeStruct((pblk, BS, share), jnp.float32),
            jax.ShapeDtypeStruct((ndiag, width), jnp.float32),
        ),
        in_specs=[SMEM, SMEM, SMEM, SMEM, VMEM, VMEM, ANY, ANY],
        out_specs=(ANY, VMEM, VMEM),
        scratch_shapes=[
            whole, whole, whole, whole, pltpu.VMEM((rows // BS, BS, share), jnp.float32),
            square, square, block, block,
            pltpu.VMEM((4, BS, BS), jnp.float32),
            pltpu.VMEM((BS, width), jnp.float32),
            pltpu.VMEM((2 * BS, width), jnp.float32),
            pltpu.VMEM((width, 2 * BS), jnp.bfloat16),
            pltpu.VMEM((width, 2 * BS), jnp.bfloat16),
            pltpu.VMEM((4,) + mask.shape, jnp.float32),
            pltpu.VMEM((4,) + mask.shape, jnp.float32),
            pltpu.VMEM((2, tile, share), jnp.float32),
            pltpu.VMEM((4, pblk, BS, share), jnp.float32),
            pltpu.VMEM((2, half, BS, share), jnp.float32),
            pltpu.VMEM((2, half, BS, share), jnp.float32),
            pltpu.VMEM((half, BS, share), jnp.float32),
            pltpu.VMEM((half, BS, share), jnp.float32),
            sems((7,)), sems((7,)),
            sems((chunks,)), sems((chunks,)), sems((chunks,)), sems((chunks,)),
            sems, sems, sems((2,)), sems((2,)), sems((3,)), sems((3,)),
            sems((4,)), sems((2,)), sems((2,)),
            sems((2, parts)), sems((2, parts)), sems((2, parts)), sems((2, parts)),
            sems((parts,)), sems((parts,)), sems((parts,)), sems((parts,)),
        ],
        compiler_params=pltpu.CompilerParams(
            collective_id=0, has_side_effects=True, vmem_limit_bytes=58 * 2**20),
        name="gather_factor",
    )(*chains, diag, mask, panel, contribution.reshape(rows // BS, BS, share))


def split(value):
    high = value.astype(jnp.bfloat16)
    return high, (value - high.astype(jnp.float32)).astype(jnp.bfloat16)


def route_slots(m, r, y, dev_y, dev_z, fill, t_ref, out_ref, ra, rb, ra2, rb2,
                asend, arecv, bsend, brecv, a2send, a2recv, b2send, b2recv):
    slots = t_ref.shape[1]
    half = slots // 2
    n = 4
    parts = half // n
    over_a, over_b, last = {}, {}, {}
    for rel in range(2):
        for k in range(parts):
            h = (1 - m) if rel == 0 else m
            over_a[rel, k] = remote(
                t_ref.at[h * 2 + y, pl.ds(k * n, n)], ra.at[rel, pl.ds(k * n, n)],
                asend.at[rel, k], arecv.at[rel, k], dev_y)
            rr = y if rel == 0 else r
            over_b[rel, k] = remote(
                t_ref.at[(1 - m) * 2 + rr, pl.ds(half + k * n, n)], rb.at[rel, pl.ds(k * n, n)],
                bsend.at[rel, k], brecv.at[rel, k], dev_z)
    fill(1 - m, y, 0, slots)
    for k in range(parts):
        over_a[0, k].start()
        over_b[0, k].start()
    fill(m, y, 0, slots)
    fill(1 - m, r, 0, slots)
    for k in range(parts):
        over_a[1, k].start()
        over_b[1, k].start()
    fill(m, r, 0, slots)
    for k in range(parts):
        part = pl.ds(k * n, n)
        other = pl.ds(half + k * n, n)
        over_a[0, k].wait_recv()
        ra[0, part] = ra[0, part] + t_ref[(1 - m) * 2 + r, part]
        over_b[0, k].wait_recv()
        rb[0, part] = rb[0, part] + t_ref[m * 2 + y, other]
        last[0, k] = remote(ra.at[0, part], ra2.at[part], a2send.at[k], a2recv.at[k], dev_z)
        last[1, k] = remote(rb.at[0, part], rb2.at[part], b2send.at[k], b2recv.at[k], dev_y)
        last[0, k].start()
        last[1, k].start()
    for k in range(parts):
        part = pl.ds(k * n, n)
        other = pl.ds(half + k * n, n)
        over_a[1, k].wait_recv()
        out_ref[part] = t_ref[m * 2 + r, part] + ra[1, part]
        over_b[1, k].wait_recv()
        out_ref[other] = t_ref[m * 2 + r, other] + rb[1, part]
    for k in range(parts):
        part = pl.ds(k * n, n)
        other = pl.ds(half + k * n, n)
        last[0, k].wait_recv()
        out_ref[part] = out_ref[part] + ra2[part]
        last[1, k].wait_recv()
        out_ref[other] = out_ref[other] + rb2[part]
    for copy in list(over_a.values()) + list(over_b.values()) + list(last.values()):
        copy.wait_send()


def on_small(diag_block, panel, pattern, contribution, route, slot):
    rows, share = panel.shape[1:]
    blk = rows // BS
    pblk = blk // 2
    nrow = lax.axis_size("row")
    mask = jnp.broadcast_to(pattern[0].astype(jnp.float32), (blk, share))
    goal = (route[0, :, 0] * pblk + slot[0]).astype(jnp.int32)
    ids = jnp.arange(blk, dtype=jnp.int32)
    earlier = (goal[None, :] == goal[:, None]) & (ids[None, :] < ids[:, None])
    prev = jnp.max(jnp.where(earlier, ids[None, :] + 1, 0), axis=1)
    names = jnp.arange(2 * nrow * pblk, dtype=jnp.int32)
    last = jnp.max(jnp.where(goal[None, :] == names[:, None], ids[None, :] + 1, 0), axis=1)
    chains = (
        jnp.maximum(prev - 1, 0), jnp.minimum(prev, 1).astype(jnp.float32),
        jnp.maximum(last - 1, 0), jnp.minimum(last, 1).astype(jnp.float32),
    )
    factor, assembled, lower = factor_and_route(
        chains, diag_block[0], mask, panel[0], contribution[0], pblk)
    return (lower[None], factor[None], assembled.reshape(1, pblk * BS, share))


def from_root(value, axis, root):
    mine = lax.axis_index(axis) == root
    return lax.psum(jnp.where(mine, value, jnp.zeros_like(value)), axis)


def partner(value, axis, apart):
    mask = 2**apart
    pairs = [(source, source ^ mask) for source in range(lax.axis_size(axis))]
    return lax.ppermute(value, axis, pairs)


def on_large(diag_block, panel, pattern, contribution, route, slot):
    highest = lax.Precision.HIGHEST
    contract = (((1,), (1,)), ((), ()))
    whole = lax.all_gather(diag_block, ("row", "col"), axis=1, tiled=True)[0]
    width = whole.shape[0]
    lower = jnp.linalg.cholesky(whole)
    inverse = jax.scipy.linalg.solve_triangular(
        lower, jnp.eye(width, dtype=jnp.float32), lower=True
    )
    ncol = lax.axis_size("col")
    nrow = lax.axis_size("row")
    col_index = lax.axis_index("col")
    tile_mask = jnp.repeat(jnp.repeat(pattern[0], BS, axis=0), BS, axis=1).astype(jnp.float32)
    masked = panel[0] * tile_mask
    rows_dev = masked.shape[0]
    full_rows = lax.all_gather(masked, "col", axis=1, tiled=True)
    factor_rows = lax.dot_general(full_rows, inverse, contract, precision=highest)
    share = width // ncol
    own_cols = lax.dynamic_slice_in_dim(factor_rows, col_index * share, share, 1)
    cw_dev = contribution.shape[2]
    head_piece = lax.dynamic_slice_in_dim(factor_rows, col_index * cw_dev, cw_dev, 0)
    head_rows = from_root(head_piece, "row", 0)
    update = contribution[0] - lax.dot_general(factor_rows, head_rows, contract, precision=highest)
    blk = rows_dev // BS
    cap = max(2, blk // nrow)
    pblk = blk // 2
    blocks = update.reshape(blk, BS * cw_dev)
    target = route[0, :, 0]
    place = slot[0]
    order_ids = jnp.arange(blk, dtype=jnp.int32)
    earlier = (target[None, :] == target[:, None]) & (order_ids[None, :] < order_ids[:, None])
    rank = jnp.sum(earlier.astype(jnp.int32), axis=1)
    half = target // nrow
    target_row = target % nrow
    position = target_row * (2 * cap) + half * cap + rank
    slots_all = jnp.arange(nrow * 2 * cap, dtype=jnp.int32)
    onehot = (position[None, :] == slots_all[:, None]).astype(jnp.float32)
    packed = jnp.dot(onehot, blocks, precision=highest).reshape(nrow, 2, cap, BS * cw_dev)
    labels = jnp.dot(onehot, (place + 1).astype(jnp.float32), precision=highest).reshape(
        nrow, 2, cap
    )
    mine = lax.axis_index("cube") % 2
    got, got_labels = (
        lax.all_to_all(packed, "row", split_axis=0, concat_axis=0, tiled=True),
        lax.all_to_all(labels, "row", split_axis=0, concat_axis=0, tiled=True),
    )
    keep = lax.dynamic_index_in_dim(got, mine, 1, keepdims=False)
    keep_labels = lax.dynamic_index_in_dim(got_labels, mine, 1, keepdims=False)
    other = lax.dynamic_index_in_dim(got, 1 - mine, 1, keepdims=False)
    other_labels = lax.dynamic_index_in_dim(got_labels, 1 - mine, 1, keepdims=False)
    back, back_labels = partner((other, other_labels), "cube", 0)
    incoming = jnp.concatenate([keep, back], axis=0).reshape(-1, BS * cw_dev)
    tags = jnp.concatenate([keep_labels, back_labels], axis=0).reshape(-1)
    wanted = jnp.arange(1, pblk + 1, dtype=jnp.float32)
    select = (tags[None, :] == wanted[:, None]).astype(jnp.float32)
    assembled = jnp.dot(select, incoming, precision=highest).reshape(pblk * BS, cw_dev)
    rows_here = diag_block.shape[1]
    diag_rows = lax.dynamic_slice_in_dim(
        lower, lax.axis_index(("row", "col")) * rows_here, rows_here, 0
    )
    return (diag_rows[None], own_cols[None], assembled[None])


def solution(mesh):
    small = mesh.shape["row"] == 2 and mesh.shape["col"] == 4
    return jax.shard_map(
        on_small if small else on_large,
        mesh=mesh,
        in_specs=(
            P("cube", ("row", "col"), None),
            P("cube", "row", "col"),
            P("cube", "row", "col"),
            P("cube", "row", "col"),
            P("cube", "row", None),
            P("cube", "row"),
        ),
        out_specs=(
            P("cube", ("row", "col"), None),
            P("cube", "row", "col"),
            P("cube", "row", "col"),
        ),
        check_vma=False,
    )
```

profile of v0, /device:TPU:0, one launch (start us, length us, event | category | flops | bytes accessed | tf_op | source)
XLA Modules:
  0.0 186.1 jit_solution(10369550597107251963)
XLA Ops:
  0.6 0.7 fusion.1
  1.3 0.7 convert_bitcast_fusion
  2.0 0.7 bitcast_add_fusion
  2.6 0.2 select_reduce_fusion.1
  2.8 0.1 select_reduce_fusion
  2.9 0.5 minimum_convert_fusion
  3.5 0.5 minimum_convert_fusion.1
  4.0 0.7 broadcast_in_dim.47.mask_ref
  4.7 173.9 %gather_factor.1 = (f32[8192,128]{1,0:T(8,128)}, f32[32,128,128]{2,1,0:T(8,128)}, f32[64,512]{1,0:T(8,128)}) custom-call(s32[64]{0:T(128)} %get-tuple-element.12.prev_ref, f32[64]{0:T(128)} %get-tuple-element.11.prev_on, s32[128]{0:T(128)} %get-tuple-element.10.last_ref, f32[128]{0:T(128)} %get-tuple-element.9.last_on, f32[64,512]{1,0:T(8,128)} %bitcast.22, ...), custom_call_target="tpu_custom_call" | custom-call | tf_op jit(solution)/shard_map/gather_factor/pallas_call | solution.py:297
  178.5 1.6 copy.12
  180.1 0.0 copy-start
  180.1 4.6 %copy.13 = f32[1,8192,128]{2,1,0:T(8,128)} copy(f32[1,8192,128]{2,1,0:T(8,128)} %bitcast.20) | data formatting | bytes 8388608
  184.7 0.0 copy-done
  184.7 1.3 copy.14
Async XLA Ops:
  180.1 4.6 %copy-start = (f32[32,128,128]{2,1,0:T(8,128)S(1)}, f32[32,128,128]{2,1,0:T(8,128)}, u32[]{:S(2)}) copy-start(f32[32,128,128]{2,1,0:T(8,128)} %get-tuple-element.8) | copy-start | bytes 6291460
where the time goes:
time: 186 us
  Pallas kernels  174 us (94%)
  local copies, waits for them, and re-layouts  8.2 us (4%)
  other arithmetic  3.34 us (2%)
    pallas_call x1, Pallas kernels, factor_and_route(): pl.pallas_call(functools.partial(gather_kernel, chunks), out_shape=(piece...  174 us
    unnamed x5, local copies, waits for them, and re-layouts  7.51 us

commit v1 on v0

v1 whole, which is shorter than its diff:
```python
import functools

import jax
import jax.numpy as jnp
from jax import lax
from jax.experimental import pallas as pl
from jax.experimental.pallas import tpu as pltpu
from jax.sharding import PartitionSpec as P

BS = 128
HIGHEST = lax.Precision.HIGHEST
NT = (((1,), (1,)), ((), ()))
ANY = pl.BlockSpec(memory_space=pl.ANY)
VMEM = pl.BlockSpec(memory_space=pltpu.VMEM)
SMEM = pl.BlockSpec(memory_space=pltpu.SMEM)
MESH = pl.DeviceIdType.MESH


def remote(src, dst, send, recv, device):
    return pltpu.make_async_remote_copy(
        src_ref=src, dst_ref=dst, send_sem=send, recv_sem=recv,
        device_id=device, device_id_type=MESH,
    )


def column(s, j):
    return jnp.take_along_axis(s, jnp.full(s.shape, j, jnp.int32), axis=1)


def factor_block(s_ref, x_ref):
    n = BS
    sub = lax.broadcasted_iota(jnp.int32, (n, n), 0)
    lane = lax.broadcasted_iota(jnp.int32, (n, n), 1)
    s = s_ref[...]
    x = (sub == lane).astype(jnp.float32)
    for k in range(n // 8):
        row = lax.broadcasted_iota(jnp.int32, s.shape, 0)
        for t in range(0, 8, 2):
            c0, c1 = column(s, 8 * k + t), column(s, 8 * k + t + 1)
            s0, s1, x0, x1 = s[t:t + 1], s[t + 1:t + 2], x[t:t + 1], x[t + 1:t + 2]
            a, b, d = c0[t:t + 1], c1[t:t + 1], c1[t + 1:t + 2]
            inv = 1.0 / (a * d - b * b)
            below = row > t + 1
            m0 = jnp.where(below, (c0 * d - c1 * b) * inv, jnp.where(row == t + 1, b / a, 0.0))
            m1 = jnp.where(below, (c1 * a - c0 * b) * inv, 0.0)
            s = s - (m0 * s0 + m1 * s1)
            x = x - (m0 * x0 + m1 * x1)
        s_ref[8 * k:8 * k + 8, :] = s[:8]
        x_ref[8 * k:8 * k + 8, :] = x[:8]
        s, x = s[8:], x[8:]


def cholesky_inverse(a_ref, inv_ref, s_ref, x_ref, between):
    width = a_ref.shape[0]
    sub = lax.broadcasted_iota(jnp.int32, (BS, BS), 0)
    lane = lax.broadcasted_iota(jnp.int32, (BS, BS), 1)
    inv_ref[...] = jnp.zeros_like(inv_ref)
    for p in range(width // BS):
        o, e = p * BS, (p + 1) * BS
        s_ref[...] = a_ref[o:e, o:e]
        factor_block(s_ref, x_ref)
        s = s_ref[...]
        d = jnp.sum(jnp.where(lane == sub, s, 0.0), axis=1, keepdims=True)
        rs = 1.0 / jnp.sqrt(d)
        low = jnp.transpose(jnp.where(lane >= sub, s, 0.0) * rs)
        x = x_ref[...] * rs
        a_ref[o:e, o:e] = low
        inv_ref[o:e, o:e] = x
        if e < width:
            below = lax.dot_general(a_ref[e:, o:e], x, NT, precision=HIGHEST)
            a_ref[e:, o:e] = below
            a_ref[e:, e:] = a_ref[e:, e:] - lax.dot_general(below, below, NT, precision=HIGHEST)
            a_ref[o:e, e:] = jnp.zeros((BS, width - e), jnp.float32)
        if p > 0:
            part = jnp.dot(a_ref[o:e, :o], inv_ref[:o, :o], precision=HIGHEST)
            inv_ref[o:e, :o] = -jnp.dot(x, part, precision=HIGHEST)
        between(p)


def gather_kernel(rows, prev_ref, prev_on, last_ref, last_on, diag_ref, mask_ref, panel_ref, contribution_ref,
                  f_ref, out_ref, l_ref,
                  own, g0, g1, g2, contrib, a_ref, inv_ref, s_ref, x_ref, h_ref, hc_ref, w_ref,
                  vh_ref, vl_ref, masks, head_masks, upd, t_ref, ra, rb, ra2, rb2,
                  dsend, drecv, xsend, xrecv, fsend, frecv, psend, precv, hsend, hrecv,
                  msend, mrecv, isem, asend, arecv, bsend, brecv, lsend, lrecv):
    z = lax.axis_index("cube")
    m = z % 2
    r, c = lax.axis_index("row"), lax.axis_index("col")
    y = 1 - r
    c1 = c + 1 - 2 * (c % 2)
    c2 = (c + 2) % 4
    c3 = (c1 + 2) % 4
    order = (c, c1, c2, c3)
    pieces = (own, g0, g1, g2)
    ndiag = diag_ref.shape[0]
    blocks = panel_ref.shape[0]
    slices = BS // rows
    slots = out_ref.shape[0]
    half = slots // 2
    heads = a_ref.shape[0] // BS
    to_x, to_core, to_row = {"col": c2}, {"col": c1}, {"row": y}
    to_cube = {"cube": z + 1 - 2 * m}

    load_own = pltpu.make_async_copy(panel_ref, own, isem.at[0])
    load_contrib = pltpu.make_async_copy(contribution_ref, contrib, isem.at[1])
    barrier = pltpu.get_barrier_semaphore()
    for device in (to_x, to_core, to_row, to_cube):
        pl.semaphore_signal(barrier, inc=1, device_id=device, device_id_type=MESH)
    pl.semaphore_wait(barrier, 4)

    def spot(rr, cc):
        return a_ref.at[pl.ds(pl.multiple_of((rr * 4 + cc) * ndiag, ndiag), ndiag)]

    def diag_copy(k, src, rr, cc, device):
        return remote(src, spot(rr, cc), dsend.at[k], drecv.at[k], device)

    def sliced(i):
        return (pl.ds(heads, blocks - heads), pl.ds(pl.multiple_of(i * rows, rows), rows))

    top = (pl.ds(0, heads),)

    def across(i, part):
        return remote(panel_ref.at[part], g1.at[part], xsend.at[i], xrecv.at[i], to_x)

    def onward(i, part):
        return remote(g1.at[part], g2.at[part], fsend.at[i], frecv.at[i], to_core)

    def beside(i, part):
        return remote(panel_ref.at[part], g0.at[part], psend.at[i], precv.at[i], to_core)

    mask_x = remote(mask_ref, masks.at[2], msend.at[0], mrecv.at[0], to_x)
    mask_core = remote(mask_ref, masks.at[1], msend.at[1], mrecv.at[1], to_core)
    mask_on = remote(masks.at[2], masks.at[3], msend.at[2], mrecv.at[2], to_core)

    first = diag_copy(0, diag_ref, r, c, to_x)
    first.start()
    mask_x.start()
    across(slices, top).start()
    for i in range(slices):
        across(i, sliced(i)).start()
    second = [diag_copy(1, diag_ref, r, c, to_row)]
    second[0].start()
    mask_core.start()
    load_own.start()
    load_contrib.start()
    a_ref[pl.ds(pl.multiple_of((r * 4 + c) * ndiag, ndiag), ndiag), :] = diag_ref[...]
    masks[0] = mask_ref[...]
    first.wait_recv()
    second.append(diag_copy(2, spot(r, c2), r, c2, to_row))
    second[1].start()
    third = [
        diag_copy(3, diag_ref, r, c, to_core),
        diag_copy(4, spot(r, c2), r, c2, to_core),
    ]
    for copy in third:
        copy.start()
    mask_x.wait_recv()
    mask_on.start()
    for copy in second:
        copy.wait_recv()
    third.append(diag_copy(5, spot(y, c), y, c, to_core))
    third.append(diag_copy(6, spot(y, c2), y, c2, to_core))
    for copy in third[2:]:
        copy.start()
    for copy in third:
        copy.wait_recv()
    for copy in [first] + second + third:
        copy.wait_send()
    beside(slices, top).start()
    across(slices, top).wait_recv()
    onward(slices, top).start()
    for i in range(slices):
        beside(i, sliced(i)).start()
    head = [remote(piece.at[c], h_ref.at[j], hsend.at[j], hrecv.at[j], to_row) for j, piece in enumerate(pieces)]
    head_mask = remote(masks, head_masks, hsend.at[4], hrecv.at[4], to_row)

    def between(p):
        if p != 0:
            return
        load_own.wait()
        load_contrib.wait()
        beside(slices, top).wait_recv()
        onward(slices, top).wait_recv()
        mask_core.wait_recv()
        mask_on.wait_recv()

        @pl.when(r == 0)
        def _():
            for copy in head:
                copy.start()
            head_mask.start()
            for j, k in enumerate(order):
                hc_ref[:, pl.ds(pl.multiple_of(k * BS, BS), BS)] = pieces[j][c] * masks[j, pl.ds(c, 1), :]

    cholesky_inverse(a_ref, inv_ref, s_ref, x_ref, between)
    l_ref[...] = a_ref[pl.ds(pl.multiple_of((r * 4 + c) * ndiag, ndiag), ndiag), :]

    @pl.when(r == 0)
    def _():
        for copy in head:
            copy.wait_send()
        head_mask.wait_send()

    @pl.when(r == 1)
    def _():
        for copy in head:
            copy.wait_recv()
        head_mask.wait_recv()
        for j, k in enumerate(order):
            hc_ref[:, pl.ds(pl.multiple_of(k * BS, BS), BS)] = h_ref[j] * head_masks[j, pl.ds(c, 1), :]

    factor_head = lax.dot_general(hc_ref[...], inv_ref[...], NT, precision=HIGHEST)
    w_ref[pl.ds(BS, BS), :] = jnp.dot(factor_head, inv_ref[...], precision=HIGHEST)
    w_ref[pl.ds(0, BS), :] = inv_ref[pl.ds(pl.multiple_of(c * BS, BS), BS), :]
    for j, k in enumerate(order):
        high, low = split(jnp.transpose(w_ref[:, pl.ds(pl.multiple_of(k * BS, BS), BS)]))
        vh_ref[j * BS:(j + 1) * BS, :] = high
        vl_ref[j * BS:(j + 1) * BS, :] = low

    group = min(blocks, 512 // rows)

    def compute(i):
        part = pl.ds(pl.multiple_of(i * rows, rows), rows)

        def tile(q, carry):
            lines = []
            for b in range(group):
                at = q * group + b
                lines.append(jnp.concatenate(
                    [piece[at, part] * masks[j, pl.ds(at, 1), :] for j, piece in enumerate(pieces)], axis=1))
            high, low = split(jnp.concatenate(lines, axis=0))
            dot = functools.partial(jnp.dot, preferred_element_type=jnp.float32)
            out = dot(high, vh_ref[...]) + (dot(high, vl_ref[...]) + dot(low, vh_ref[...]))
            for b in range(group):
                at = q * group + b
                f_ref[at, part] = out[b * rows:(b + 1) * rows, :BS]
                update = contrib[at, part] - out[b * rows:(b + 1) * rows, BS:]
                upd[at] = update + prev_on[at] * upd[prev_ref[at]]
            return carry

        lax.fori_loop(0, blocks // group, tile, 0)

        def fill(q, carry):
            for b in range(8):
                k = q * 8 + b
                t_ref[k, part] = upd[last_ref[k]] * last_on[k]
            return carry

        lax.fori_loop(0, 4 * slots // 8, fill, 0)

    def quarter(g, low):
        return pl.ds(g * slots + (0 if low else half), half)

    def hops(i):
        part = pl.ds(pl.multiple_of(i * rows, rows), rows)
        goal = ((1 - m) * 2 + y, m * 2 + y, (1 - m) * 2 + r)
        over_a = [remote(t_ref.at[quarter(goal[k], True), part], ra.at[k, :, part],
                         asend.at[k, i], arecv.at[k, i], to_row) for k in range(2)]
        over_b = [remote(t_ref.at[quarter(goal[2 * k], False), part], rb.at[k, :, part],
                         bsend.at[k, i], brecv.at[k, i], to_cube) for k in range(2)]
        last = [remote(ra.at[0, :, part], ra2.at[:, part], lsend.at[0, i], lrecv.at[0, i], to_cube),
                remote(rb.at[0, :, part], rb2.at[:, part], lsend.at[1, i], lrecv.at[1, i], to_row)]
        return part, over_a, over_b, last

    def turn(i):
        part, over_a, over_b, last = hops(i)
        over_a[0].wait_recv()
        ra[0, :, part] = ra[0, :, part] + t_ref[quarter((1 - m) * 2 + r, True), part]
        last[0].start()
        over_b[0].wait_recv()
        rb[0, :, part] = rb[0, :, part] + t_ref[quarter(m * 2 + y, False), part]
        last[1].start()

    def finish(i):
        part, over_a, over_b, last = hops(i)
        over_a[1].wait_recv()
        last[0].wait_recv()
        out_ref[pl.ds(0, half), part] = t_ref[quarter(m * 2 + r, True), part] + ra[1, :, part] + ra2[:, part]
        over_b[1].wait_recv()
        last[1].wait_recv()
        out_ref[pl.ds(half, half), part] = t_ref[quarter(m * 2 + r, False), part] + rb[1, :, part] + rb2[:, part]

    upd[...] = jnp.zeros_like(upd)

    def step(i, carry):
        @pl.when(i < slices)
        def _():
            across(i, sliced(i)).wait_recv()
            onward(i, sliced(i)).start()
            beside(i, sliced(i)).wait_recv()
            onward(i, sliced(i)).wait_recv()
            compute(i)
            _, over_a, over_b, _ = hops(i)
            for k in range(2):
                over_a[k].start()
                over_b[k].start()

        @pl.when((i > 0) & (i <= slices))
        def _():
            turn(i - 1)

        @pl.when(i > 1)
        def _():
            finish(i - 2)
        return carry

    lax.fori_loop(0, slices + 2, step, 0)

    def drain(i, carry):
        _, over_a, over_b, last = hops(i)
        for copy in over_a + over_b + last + [across(i, sliced(i)), onward(i, sliced(i)), beside(i, sliced(i))]:
            copy.wait_send()
        return carry

    lax.fori_loop(0, slices, drain, 0)
    for copy in (across(slices, top), onward(slices, top), beside(slices, top), mask_x, mask_core, mask_on):
        copy.wait_send()


def factor_and_route(chains, diag, mask, panel, contribution, pblk):
    rows = 16
    slices = BS // rows
    tall, share = panel.shape
    blk = tall // BS
    half = pblk // 2
    ndiag, width = diag.shape
    whole = pltpu.VMEM((blk, BS, share), jnp.float32)
    square = pltpu.VMEM((width, width), jnp.float32)
    block = pltpu.VMEM((BS, BS), jnp.float32)
    sems = pltpu.SemaphoreType.DMA
    return pl.pallas_call(
        functools.partial(gather_kernel, rows),
        out_shape=(
            jax.ShapeDtypeStruct((blk, BS, share), jnp.float32),
            jax.ShapeDtypeStruct((pblk, BS, share), jnp.float32),
            jax.ShapeDtypeStruct((ndiag, width), jnp.float32),
        ),
        in_specs=[SMEM, SMEM, SMEM, SMEM, VMEM, VMEM, ANY, ANY],
        out_specs=(VMEM, VMEM, VMEM),
        scratch_shapes=[
            whole, whole, whole, whole, whole,
            square, square, block, block,
            pltpu.VMEM((4, BS, BS), jnp.float32),
            pltpu.VMEM((BS, width), jnp.float32),
            pltpu.VMEM((2 * BS, width), jnp.float32),
            pltpu.VMEM((width, 2 * BS), jnp.bfloat16),
            pltpu.VMEM((width, 2 * BS), jnp.bfloat16),
            pltpu.VMEM((4,) + mask.shape, jnp.float32),
            pltpu.VMEM((4,) + mask.shape, jnp.float32),
            pltpu.VMEM((blk, rows, share), jnp.float32),
            pltpu.VMEM((4 * pblk, BS, share), jnp.float32),
            pltpu.VMEM((2, half, BS, share), jnp.float32),
            pltpu.VMEM((2, half, BS, share), jnp.float32),
            pltpu.VMEM((half, BS, share), jnp.float32),
            pltpu.VMEM((half, BS, share), jnp.float32),
            sems((7,)), sems((7,)),
            sems((slices + 1,)), sems((slices + 1,)), sems((slices + 1,)), sems((slices + 1,)),
            sems((slices + 1,)), sems((slices + 1,)), sems((5,)), sems((5,)), sems((3,)), sems((3,)),
            sems((2,)),
            sems((2, slices)), sems((2, slices)), sems((2, slices)), sems((2, slices)),
            sems((2, slices)), sems((2, slices)),
        ],
        compiler_params=pltpu.CompilerParams(
            collective_id=0, has_side_effects=True, vmem_limit_bytes=54 * 2**20),
        name="gather_factor",
    )(*chains, diag, mask, panel.reshape(blk, BS, share), contribution.reshape(blk, BS, share))


def split(value):
    high = value.astype(jnp.bfloat16)
    return high, (value - high.astype(jnp.float32)).astype(jnp.bfloat16)


def on_small(diag_block, panel, pattern, contribution, route, slot):
    rows, share = panel.shape[1:]
    blk = rows // BS
    pblk = blk // 2
    nrow = lax.axis_size("row")
    mask = jnp.broadcast_to(pattern[0].astype(jnp.float32), (blk, share))
    goal = (route[0, :, 0] * pblk + slot[0]).astype(jnp.int32)
    ids = jnp.arange(blk, dtype=jnp.int32)
    earlier = (goal[None, :] == goal[:, None]) & (ids[None, :] < ids[:, None])
    prev = jnp.max(jnp.where(earlier, ids[None, :] + 1, 0), axis=1)
    names = jnp.arange(2 * nrow * pblk, dtype=jnp.int32)
    last = jnp.max(jnp.where(goal[None, :] == names[:, None], ids[None, :] + 1, 0), axis=1)
    chains = (
        jnp.maximum(prev - 1, 0), jnp.minimum(prev, 1).astype(jnp.float32),
        jnp.maximum(last - 1, 0), jnp.minimum(last, 1).astype(jnp.float32),
    )
    factor, assembled, lower = factor_and_route(
        chains, diag_block[0], mask, panel[0], contribution[0], pblk)
    return (lower[None], factor.reshape(1, rows, share), assembled.reshape(1, pblk * BS, share))


def from_root(value, axis, root):
    mine = lax.axis_index(axis) == root
    return lax.psum(jnp.where(mine, value, jnp.zeros_like(value)), axis)


def partner(value, axis, apart):
    mask = 2**apart
    pairs = [(source, source ^ mask) for source in range(lax.axis_size(axis))]
    return lax.ppermute(value, axis, pairs)


def on_large(diag_block, panel, pattern, contribution, route, slot):
    highest = lax.Precision.HIGHEST
    contract = (((1,), (1,)), ((), ()))
    whole = lax.all_gather(diag_block, ("row", "col"), axis=1, tiled=True)[0]
    width = whole.shape[0]
    lower = jnp.linalg.cholesky(whole)
    inverse = jax.scipy.linalg.solve_triangular(
        lower, jnp.eye(width, dtype=jnp.float32), lower=True
    )
    ncol = lax.axis_size("col")
    nrow = lax.axis_size("row")
    col_index = lax.axis_index("col")
    tile_mask = jnp.repeat(jnp.repeat(pattern[0], BS, axis=0), BS, axis=1).astype(jnp.float32)
    masked = panel[0] * tile_mask
    rows_dev = masked.shape[0]
    full_rows = lax.all_gather(masked, "col", axis=1, tiled=True)
    factor_rows = lax.dot_general(full_rows, inverse, contract, precision=highest)
    share = width // ncol
    own_cols = lax.dynamic_slice_in_dim(factor_rows, col_index * share, share, 1)
    cw_dev = contribution.shape[2]
    head_piece = lax.dynamic_slice_in_dim(factor_rows, col_index * cw_dev, cw_dev, 0)
    head_rows = from_root(head_piece, "row", 0)
    update = contribution[0] - lax.dot_general(factor_rows, head_rows, contract, precision=highest)
    blk = rows_dev // BS
    cap = max(2, blk // nrow)
    pblk = blk // 2
    blocks = update.reshape(blk, BS * cw_dev)
    target = route[0, :, 0]
    place = slot[0]
    order_ids = jnp.arange(blk, dtype=jnp.int32)
    earlier = (target[None, :] == target[:, None]) & (order_ids[None, :] < order_ids[:, None])
    rank = jnp.sum(earlier.astype(jnp.int32), axis=1)
    half = target // nrow
    target_row = target % nrow
    position = target_row * (2 * cap) + half * cap + rank
    slots_all = jnp.arange(nrow * 2 * cap, dtype=jnp.int32)
    onehot = (position[None, :] == slots_all[:, None]).astype(jnp.float32)
    packed = jnp.dot(onehot, blocks, precision=highest).reshape(nrow, 2, cap, BS * cw_dev)
    labels = jnp.dot(onehot, (place + 1).astype(jnp.float32), precision=highest).reshape(
        nrow, 2, cap
    )
    mine = lax.axis_index("cube") % 2
    got, got_labels = (
        lax.all_to_all(packed, "row", split_axis=0, concat_axis=0, tiled=True),
        lax.all_to_all(labels, "row", split_axis=0, concat_axis=0, tiled=True),
    )
    keep = lax.dynamic_index_in_dim(got, mine, 1, keepdims=False)
    keep_labels = lax.dynamic_index_in_dim(got_labels, mine, 1, keepdims=False)
    other = lax.dynamic_index_in_dim(got, 1 - mine, 1, keepdims=False)
    other_labels = lax.dynamic_index_in_dim(got_labels, 1 - mine, 1, keepdims=False)
    back, back_labels = partner((other, other_labels), "cube", 0)
    incoming = jnp.concatenate([keep, back], axis=0).reshape(-1, BS * cw_dev)
    tags = jnp.concatenate([keep_labels, back_labels], axis=0).reshape(-1)
    wanted = jnp.arange(1, pblk + 1, dtype=jnp.float32)
    select = (tags[None, :] == wanted[:, None]).astype(jnp.float32)
    assembled = jnp.dot(select, incoming, precision=highest).reshape(pblk * BS, cw_dev)
    rows_here = diag_block.shape[1]
    diag_rows = lax.dynamic_slice_in_dim(
        lower, lax.axis_index(("row", "col")) * rows_here, rows_here, 0
    )
    return (diag_rows[None], own_cols[None], assembled[None])


def solution(mesh):
    small = mesh.shape["row"] == 2 and mesh.shape["col"] == 4
    return jax.shard_map(
        on_small if small else on_large,
        mesh=mesh,
        in_specs=(
            P("cube", ("row", "col"), None),
            P("cube", "row", "col"),
            P("cube", "row", "col"),
            P("cube", "row", "col"),
            P("cube", "row", None),
            P("cube", "row"),
        ),
        out_specs=(
            P("cube", ("row", "col"), None),
            P("cube", "row", "col"),
            P("cube", "row", "col"),
        ),
        check_vma=False,
    )
```

time: 186 us -> 133 us (0.72)
  Pallas kernels: 174 us -> 120 us
    pallas_call x1, Pallas kernels: 174 us -> 120 us  [factor_and_route(): pl.pallas_call(functools.partial(gather_kernel, rows), out_shape=(jax.Sha...]
where the time goes in v1:
time: 133 us
  Pallas kernels  120 us (90%)
  local copies, waits for them, and re-layouts  8.2 us (6%)
  other arithmetic  3.34 us (3%)
    pallas_call x1, Pallas kernels, factor_and_route(): pl.pallas_call(functools.partial(gather_kernel, rows), out_shape=(jax.Sha...  120 us
    unnamed x5, local copies, waits for them, and re-layouts  7.51 us

profile of v1, /device:TPU:0, one launch (start us, length us, event | category | flops | bytes accessed | tf_op | source)
XLA Modules:
  0.0 132.6 jit_solution(6292435906649465990)
XLA Ops:
  0.6 0.7 fusion.1
  1.3 0.7 convert_bitcast_fusion
  2.0 0.7 bitcast_add_fusion
  2.6 0.2 select_reduce_fusion.1
  2.8 0.1 select_reduce_fusion
  2.9 0.5 minimum_convert_fusion
  3.5 0.5 minimum_convert_fusion.1
  4.0 0.7 broadcast_in_dim.44.mask_ref
  4.7 120.4 %gather_factor.1 = (f32[64,128,128]{2,1,0:T(8,128)}, f32[32,128,128]{2,1,0:T(8,128)}, f32[64,512]{1,0:T(8,128)}) custom-call(s32[64]{0:T(128)} %get-tuple-element.12.prev_ref, f32[64]{0:T(128)} %get-tuple-element.11.prev_on, s32[128]{0:T(128)} %get-tuple-element.10.last_ref, f32[128]{0:T(128)} %get-tuple-element.9.last_on, f32[64,512]{1,0:T(8,128)} %bitcast.22, ...), custom_call_target="tpu_custom_call" | custom-call | tf_op jit(solution)/shard_map/gather_factor/pallas_call | solution.py:331
  125.1 1.6 %copy.12 = f32[1,64,512]{2,1,0:T(8,128)} copy(f32[1,64,512]{2,1,0:T(8,128)} %bitcast.23) | data formatting | bytes 262144
  126.6 0.0 copy-start
  126.6 4.6 %copy.13 = f32[1,8192,128]{2,1,0:T(8,128)} copy(f32[1,8192,128]{2,1,0:T(8,128)} %bitcast.20) | data formatting | bytes 8388608
  131.3 0.0 copy-done
  131.3 1.3 copy.14
Async XLA Ops:
  126.6 4.6 %copy-start = (f32[32,128,128]{2,1,0:T(8,128)S(1)}, f32[32,128,128]{2,1,0:T(8,128)}, u32[]{:S(2)}) copy-start(f32[32,128,128]{2,1,0:T(8,128)} %get-tuple-element.8) | copy-start | bytes 6291460

commit v2 on v1

v2 whole, which is shorter than its diff:
```python
import functools

import jax
import jax.numpy as jnp
from jax import lax
from jax.experimental import pallas as pl
from jax.experimental.pallas import tpu as pltpu
from jax.sharding import PartitionSpec as P

BS = 128
HIGHEST = lax.Precision.HIGHEST
NT = (((1,), (1,)), ((), ()))
TN = (((0,), (0,)), ((), ()))
ANY = pl.BlockSpec(memory_space=pl.ANY)
VMEM = pl.BlockSpec(memory_space=pltpu.VMEM)
MESH = pl.DeviceIdType.MESH


def remote(src, dst, send, recv, device):
    return pltpu.make_async_remote_copy(
        src_ref=src, dst_ref=dst, send_sem=send, recv_sem=recv,
        device_id=device, device_id_type=MESH,
    )


def column(s, j):
    return jnp.take_along_axis(s, jnp.full(s.shape, j, jnp.int32), axis=1)


def factor_block(s_ref, x_ref, middle):
    n, w = BS, 8
    s = s_ref[...]
    for k in range(n // w):
        if k == n // w // 2:
            middle()
        o = w * k
        row = lax.broadcasted_iota(jnp.int32, (w, n), 0)
        lane = lax.broadcasted_iota(jnp.int32, (w, n), 1)
        full, rest = s[:w], s[w:]
        ct = [column(full, o + q) for q in range(w)]
        top = jnp.where((lane >= o) & (lane < o + w), (lane - o == row).astype(jnp.float32), full)
        more = o + w < n
        if more:
            cr = [column(rest, o + q) for q in range(w)]
            lanes = lax.broadcasted_iota(jnp.int32, rest.shape, 1)
            rest = jnp.where((lanes >= o) & (lanes < o + w), 0.0, rest)
        for t in range(0, w, 2):
            c0, c1 = ct[t], ct[t + 1]
            a, b, d = c0[t:t + 1], c1[t:t + 1], c1[t + 1:t + 2]
            inv = 1.0 / (a * d - b * b)
            below = row > t + 1
            m0 = jnp.where(below, (c0 * d - c1 * b) * inv, jnp.where(row == t + 1, b / a, 0.0))
            m1 = jnp.where(below, (c1 * a - c0 * b) * inv, 0.0)
            pairs = [(ct[q][t:t + 1], ct[q][t + 1:t + 2]) for q in range(w)]
            u0, u1 = top[t:t + 1], top[t + 1:t + 2]
            for q in range(t + 2, w):
                ct[q] = ct[q] - (m0 * pairs[q][0] + m1 * pairs[q][1])
            full = full - (m0 * full[t:t + 1] + m1 * full[t + 1:t + 2])
            top = top - (m0 * u0 + m1 * u1)
            if more:
                ai, bi, di = a * inv, b * inv, d * inv
                r0 = cr[t] * di - cr[t + 1] * bi
                r1 = cr[t + 1] * ai - cr[t] * bi
                for q in range(t + 2, w):
                    cr[q] = cr[q] - (r0 * pairs[q][0] + r1 * pairs[q][1])
                rest = rest - (r0 * u0 + r1 * u1)
        s_ref[o:o + w, :] = full
        x_ref[o:o + w, :] = jnp.where(lane <= row + o, top, 0.0)
        s = rest


def cholesky_inverse(a_ref, inv_ref, s_ref, x_ref, r_ref, middle, ready, between):
    width = a_ref.shape[0]
    sub = lax.broadcasted_iota(jnp.int32, (BS, BS), 0)
    lane = lax.broadcasted_iota(jnp.int32, (BS, BS), 1)
    inv_ref[...] = jnp.zeros_like(inv_ref)
    for p in range(width // BS):
        o, e = p * BS, (p + 1) * BS
        if p == 0:
            s_ref[...] = a_ref[o:e, o:e]
        else:
            left = a_ref[:o, o:e]
            s_ref[...] = a_ref[o:e, o:e] - lax.dot_general(left, left, TN, precision=HIGHEST)
            r_ref[:, :o] = -lax.dot_general(left, inv_ref[:o, :o], TN, precision=HIGHEST)
            if e < width:
                r_ref[:, e:] = a_ref[o:e, e:] - lax.dot_general(left, a_ref[:o, e:], TN, precision=HIGHEST)
        factor_block(s_ref, x_ref, middle if p == 0 else (lambda: None))
        if p == 0:
            ready()
        s = s_ref[...]
        d = jnp.sum(jnp.where(lane == sub, s, 0.0), axis=1, keepdims=True)
        rs = 1.0 / jnp.sqrt(d)
        x = x_ref[...] * rs
        a_ref[o:e, o:e] = jnp.where(lane >= sub, s, 0.0) * rs
        inv_ref[o:e, o:e] = x
        if p == 0:
            r_ref[:, e:] = a_ref[o:e, e:]
        if e < width:
            a_ref[o:e, e:] = jnp.dot(x, r_ref[:, e:], precision=HIGHEST)
        if p > 0:
            inv_ref[o:e, :o] = jnp.dot(x, r_ref[:, :o], precision=HIGHEST)
        between(p)


def to_column(row):
    n = row.shape[1]
    sub = lax.broadcasted_iota(jnp.int32, (n, n), 0)
    lane = lax.broadcasted_iota(jnp.int32, (n, n), 1)
    return jnp.sum(jnp.where(sub == lane, row, 0.0), axis=1, keepdims=True)


def chains(goal, slots, table_ref):
    n = goal.shape[1]
    sub = lax.broadcasted_iota(jnp.int32, (n, n), 0)
    lane = lax.broadcasted_iota(jnp.int32, (n, n), 1)
    goal_column = to_column(goal)
    earlier = (goal_column == goal) & (sub < lane)
    number = (sub + 1).astype(jnp.float32)
    prev = jnp.max(jnp.where(earlier, number, 0.0), axis=0, keepdims=True)
    names = lax.broadcasted_iota(jnp.int32, (n, slots), 1).astype(jnp.float32)
    number = (lax.broadcasted_iota(jnp.int32, (n, slots), 0) + 1).astype(jnp.float32)
    last = jnp.max(jnp.where(goal_column == names, number, 0.0), axis=0, keepdims=True)
    table_ref[...] = jnp.zeros_like(table_ref)
    table_ref[0:1, 0:n] = prev.astype(jnp.int32)
    table_ref[1:2, 0:slots] = last.astype(jnp.int32)


def gather_kernel(rows, route_ref, slot_ref, pattern_ref, diag_ref, panel_ref, contribution_ref,
                  f_ref, out_ref, l_ref,
                  own, g0, g1, g2, contrib, a_ref, inv_ref, s_ref, x_ref, r_ref, h_ref, hc_ref, v_ref,
                  vh_ref, vl_ref, masks, head_masks, pats, head_pats, pattern, route, slot, table, names, upd, t_ref, ra, rb, ra2, rb2,
                  dsend, drecv, xsend, xrecv, fsend, frecv, psend, precv, hsend, hrecv,
                  msend, mrecv, isem, asend, arecv, bsend, brecv, lsend, lrecv):
    z = lax.axis_index("cube")
    m = z % 2
    r, c = lax.axis_index("row"), lax.axis_index("col")
    y = 1 - r
    c1 = c + 1 - 2 * (c % 2)
    c2 = (c + 2) % 4
    c3 = (c1 + 2) % 4
    order = (c, c1, c2, c3)
    pieces = (own, g0, g1, g2)
    ndiag, width = diag_ref.shape
    blocks = panel_ref.shape[0]
    slices = BS // rows
    slots = out_ref.shape[0]
    half = slots // 2
    heads = width // BS
    to_x, to_core, to_row = {"col": c2}, {"col": c1}, {"row": y}
    to_cube = {"cube": z + 1 - 2 * m}

    def spot(rr, cc, k):
        return (pl.ds(pl.multiple_of((rr * 4 + cc) * ndiag, ndiag), ndiag),
                pl.ds(0, BS) if k == 0 else pl.ds(BS, width - BS))

    load_own = pltpu.make_async_copy(panel_ref, own, isem.at[0])
    load_contrib = pltpu.make_async_copy(contribution_ref, contrib, isem.at[1])
    load_diag = [pltpu.make_async_copy(
        diag_ref.at[:, spot(r, c, k)[1]], a_ref.at[spot(r, c, k)], isem.at[2 + k]) for k in range(2)]
    load_table = pltpu.make_async_copy(table, names, isem.at[4])
    load_small = [pltpu.make_async_copy(source, target, isem.at[5 + k]) for k, (source, target) in enumerate(
        ((pattern_ref, pattern), (route_ref, route), (slot_ref, slot)))]
    for copy in load_small + load_diag:
        copy.start()
    pats[...] = jnp.zeros_like(pats)
    barrier = pltpu.get_barrier_semaphore()
    for device in (to_x, to_core, to_row, to_cube):
        pl.semaphore_signal(barrier, inc=1, device_id=device, device_id_type=MESH)
    for copy in load_small:
        copy.wait()
    pats[0, 0:1, 0:blocks] = pattern[...].astype(jnp.float32)
    pl.semaphore_wait(barrier, 4)

    def spread(source, target):
        for j in range(4):
            target[j] = jnp.broadcast_to(to_column(source[j, 0:1, 0:blocks]), target.shape[1:])


    def piece_copy(k, n, rr, cc, device):
        part = spot(rr, cc, k)
        return remote(a_ref.at[part], a_ref.at[part], dsend.at[k, n], drecv.at[k, n], device)

    def own_copy(k, n, device):
        part = spot(r, c, k)
        return remote(diag_ref.at[:, part[1]], a_ref.at[part], dsend.at[k, n], drecv.at[k, n], device)

    diag = [(own_copy(k, 0, to_x), own_copy(k, 1, to_row), piece_copy(k, 2, r, c2, to_row),
             own_copy(k, 3, to_core), piece_copy(k, 4, r, c2, to_core), piece_copy(k, 5, y, c, to_core),
             piece_copy(k, 6, y, c2, to_core)) for k in range(2)]

    def sliced(i):
        return (pl.ds(heads, blocks - heads), pl.ds(pl.multiple_of(i * rows, rows), rows))

    top = (pl.ds(0, heads),)

    def across(i, part):
        return remote(panel_ref.at[part], g1.at[part], xsend.at[i], xrecv.at[i], to_x)

    def onward(i, part):
        return remote(g1.at[part], g2.at[part], fsend.at[i], frecv.at[i], to_core)

    def beside(i, part):
        return remote(panel_ref.at[part], g0.at[part], psend.at[i], precv.at[i], to_core)

    mask_x = remote(pats.at[0], pats.at[2], msend.at[0], mrecv.at[0], to_x)
    mask_core = remote(pats.at[0], pats.at[1], msend.at[1], mrecv.at[1], to_core)
    mask_on = remote(pats.at[2], pats.at[3], msend.at[2], mrecv.at[2], to_core)

    for k in range(2):
        for n in (0, 1, 3):
            diag[k][n].start()
    mask_x.start()
    across(slices, top).start()
    for i in range(slices):
        across(i, sliced(i)).start()
    mask_core.start()
    beside(slices, top).start()
    load_own.start()
    load_contrib.start()
    for k in range(2):
        diag[k][0].wait_recv()
        diag[k][2].start()
        diag[k][4].start()
        diag[k][1].wait_recv()
        diag[k][5].start()
        if k == 0:
            diag[k][2].wait_recv()
            diag[k][6].start()
            for n in (3, 4, 5, 6):
                diag[k][n].wait_recv()
    for copy in load_diag:
        copy.wait()

    def middle():
        diag[1][2].wait_recv()
        diag[1][6].start()

    def ready():
        for n in (3, 4, 5, 6):
            diag[1][n].wait_recv()
        for copies in diag:
            for copy in copies:
                copy.wait_send()

    head = [remote(piece.at[c], h_ref.at[j], hsend.at[j], hrecv.at[j], to_row) for j, piece in enumerate(pieces)]
    head_mask = remote(pats, head_pats, hsend.at[4], hrecv.at[4], to_row)

    def project(p):
        o, e = p * BS, (p + 1) * BS
        line = inv_ref[o:e, :e]
        part = lax.dot_general(line, hc_ref[:, :e], NT, precision=HIGHEST)
        term = lax.dot_general(line, part, TN, precision=HIGHEST)
        if o:
            v_ref[:o] = v_ref[:o] + term[:o]
        v_ref[o:e] = term[o:]

    def between(p):
        if p == 0:
            across(slices, top).wait_recv()
            onward(slices, top).start()
            mask_x.wait_recv()
            mask_on.start()
            for i in range(slices):
                beside(i, sliced(i)).start()
            chains((route[...] * slots + slot[...]).astype(jnp.float32), 4 * slots, table)
            load_table.start()
        if p == 1:
            load_own.wait()
            load_contrib.wait()
            beside(slices, top).wait_recv()
            onward(slices, top).wait_recv()
            mask_core.wait_recv()
            mask_on.wait_recv()
            spread(pats, masks)

            @pl.when(r == 0)
            def _():
                for copy in head:
                    copy.start()
                head_mask.start()
                for j, k in enumerate(order):
                    hc_ref[:, pl.ds(pl.multiple_of(k * BS, BS), BS)] = pieces[j][c] * masks[j, pl.ds(c, 1), :]

        if p == 2:
            @pl.when(r == 1)
            def _():
                for copy in head:
                    copy.wait_recv()
                head_mask.wait_recv()
                spread(head_pats, head_masks)
                for j, k in enumerate(order):
                    hc_ref[:, pl.ds(pl.multiple_of(k * BS, BS), BS)] = h_ref[j] * head_masks[j, pl.ds(c, 1), :]

            for q in range(3):
                project(q)
        if p == 3:
            project(3)

    cholesky_inverse(a_ref, inv_ref, s_ref, x_ref, r_ref, middle, ready, between)
    for j, k in enumerate(order):
        at = pl.ds(pl.multiple_of(k * BS, BS), BS)
        side = jnp.transpose(inv_ref[pl.ds(pl.multiple_of(c * BS, BS), BS), at])
        for q, value in ((0, side), (BS, v_ref[at, :])):
            high, low = split(value)
            vh_ref[j * BS:(j + 1) * BS, q:q + BS] = high
            vl_ref[j * BS:(j + 1) * BS, q:q + BS] = low

    def lower_rows():
        p = 2 * r + c // 2
        for k in range(heads):
            block = jnp.transpose(a_ref[k * BS:(k + 1) * BS, pl.ds(pl.multiple_of(p * BS, BS), BS)])
            s_ref[...] = jnp.where(k <= p, block, 0.0)
            l_ref[:, k * BS:(k + 1) * BS] = s_ref[pl.ds(pl.multiple_of((c % 2) * ndiag, ndiag), ndiag), :]

    load_table.wait()
    group = min(blocks, 512 // rows)

    def compute(i):
        part = pl.ds(pl.multiple_of(i * rows, rows), rows)

        def tile(q, carry):
            lines = []
            for b in range(group):
                at = q * group + b
                lines.append(jnp.concatenate(
                    [piece[at, part] * masks[j, pl.ds(at, 1), :] for j, piece in enumerate(pieces)], axis=1))
            high, low = split(jnp.concatenate(lines, axis=0))
            dot = functools.partial(jnp.dot, preferred_element_type=jnp.float32)
            out = dot(high, vh_ref[...]) + (dot(high, vl_ref[...]) + dot(low, vh_ref[...]))
            for b in range(group):
                at = q * group + b
                f_ref[at, part] = out[b * rows:(b + 1) * rows, :BS]
                update = contrib[at, part] - out[b * rows:(b + 1) * rows, BS:]
                name = names[0, at]
                upd[at] = update + jnp.where(name > 0, 1.0, 0.0) * upd[jnp.clip(name - 1, 0, blocks - 1)]
            return carry

        lax.fori_loop(0, blocks // group, tile, 0)

        def fill(q, carry):
            for b in range(16):
                k = q * 16 + b
                name = names[1, k]
                t_ref[i, k] = upd[jnp.clip(name - 1, 0, blocks - 1)] * jnp.where(name > 0, 1.0, 0.0)
            return carry

        lax.fori_loop(0, 4 * slots // 16, fill, 0)

    def quarter(g, low):
        return pl.ds(g * slots + (0 if low else half), half)

    def hops(i):
        goal = ((1 - m) * 2 + y, m * 2 + y, (1 - m) * 2 + r)
        over_a = [remote(t_ref.at[i, quarter(goal[k], True)], ra.at[k, i],
                         asend.at[k, i], arecv.at[k, i], to_row) for k in range(2)]
        over_b = [remote(t_ref.at[i, quarter(goal[2 * k], False)], rb.at[k, i],
                         bsend.at[k, i], brecv.at[k, i], to_cube) for k in range(2)]
        last = [remote(ra.at[0, i], ra2.at[i], lsend.at[0, i], lrecv.at[0, i], to_cube),
                remote(rb.at[0, i], rb2.at[i], lsend.at[1, i], lrecv.at[1, i], to_row)]
        return over_a, over_b, last

    def turn(i):
        over_a, over_b, last = hops(i)
        over_a[0].wait_recv()
        ra[0, i] = ra[0, i] + t_ref[i, quarter((1 - m) * 2 + r, True)]
        last[0].start()
        over_b[0].wait_recv()
        rb[0, i] = rb[0, i] + t_ref[i, quarter(m * 2 + y, False)]
        last[1].start()

    def finish(i):
        part = pl.ds(pl.multiple_of(i * rows, rows), rows)
        over_a, over_b, last = hops(i)
        over_a[1].wait_recv()
        last[0].wait_recv()
        out_ref[pl.ds(0, half), part] = t_ref[i, quarter(m * 2 + r, True)] + ra[1, i] + ra2[i]
        over_b[1].wait_recv()
        last[1].wait_recv()
        out_ref[pl.ds(half, half), part] = t_ref[i, quarter(m * 2 + r, False)] + rb[1, i] + rb2[i]

    upd[...] = jnp.zeros_like(upd)

    def step(i, carry):
        @pl.when(i == 3)
        def _():
            lower_rows()

        @pl.when(i < slices)
        def _():
            across(i, sliced(i)).wait_recv()
            onward(i, sliced(i)).start()

        @pl.when(i == slices - 1)
        def _():
            turn(i - 1)

        @pl.when(i < slices)
        def _():
            beside(i, sliced(i)).wait_recv()
            onward(i, sliced(i)).wait_recv()
            compute(i)
            over_a, over_b, _ = hops(i)
            for k in range(2):
                over_a[k].start()
                over_b[k].start()

        @pl.when((i > 0) & (i <= slices) & (i != slices - 1))
        def _():
            turn(i - 1)

        @pl.when(i > 2)
        def _():
            finish(i - 3)

        @pl.when(i > 3)
        def _():
            drain(i - 4)
        return carry

    def drain(i):
        over_a, over_b, last = hops(i)
        for copy in over_a + over_b + last + [across(i, sliced(i)), onward(i, sliced(i)), beside(i, sliced(i))]:
            copy.wait_send()

    lax.fori_loop(0, slices + 3, step, 0)

    for i in (slices - 1,):
        drain(i)
    for copy in (across(slices, top), onward(slices, top), beside(slices, top), mask_x, mask_core, mask_on):
        copy.wait_send()

    @pl.when(r == 0)
    def _():
        for copy in head:
            copy.wait_send()
        head_mask.wait_send()


def factor_and_route(route, slot, pattern, diag, panel, contribution):
    rows = 8
    slices = BS // rows
    tall, share = panel.shape
    blk = tall // BS
    pblk = blk // 2
    half = pblk // 2
    ndiag, width = diag.shape
    whole = pltpu.VMEM((blk, BS, share), jnp.float32)
    square = pltpu.VMEM((width, width), jnp.float32)
    block = pltpu.VMEM((BS, BS), jnp.float32)
    sems = pltpu.SemaphoreType.DMA
    return pl.pallas_call(
        functools.partial(gather_kernel, rows),
        out_shape=(
            pltpu.VMEM((blk, BS, share), jnp.float32),
            pltpu.VMEM((pblk, BS, share), jnp.float32),
            pltpu.VMEM((ndiag, width), jnp.float32),
        ),
        in_specs=[ANY] * 6,
        out_specs=(VMEM, VMEM, VMEM),
        scratch_shapes=[
            whole, whole, whole, whole, whole,
            square, square, block, block,
            pltpu.VMEM((BS, width), jnp.float32),
            pltpu.VMEM((4, BS, BS), jnp.float32),
            pltpu.VMEM((BS, width), jnp.float32),
            pltpu.VMEM((width, BS), jnp.float32),
            pltpu.VMEM((width, 2 * BS), jnp.bfloat16),
            pltpu.VMEM((width, 2 * BS), jnp.bfloat16),
            pltpu.VMEM((4, blk, share), jnp.float32),
            pltpu.VMEM((4, blk, share), jnp.float32),
            pltpu.VMEM((4, 8, BS), jnp.float32),
            pltpu.VMEM((4, 8, BS), jnp.float32),
            pltpu.VMEM((1, blk), jnp.int32),
            pltpu.VMEM((1, blk), jnp.int32),
            pltpu.VMEM((1, blk), jnp.int32),
            pltpu.VMEM((8, BS), jnp.int32),
            pltpu.SMEM((8, BS), jnp.int32),
            pltpu.VMEM((blk, rows, share), jnp.float32),
            pltpu.VMEM((slices, 4 * pblk, rows, share), jnp.float32),
            pltpu.VMEM((2, slices, half, rows, share), jnp.float32),
            pltpu.VMEM((2, slices, half, rows, share), jnp.float32),
            pltpu.VMEM((slices, half, rows, share), jnp.float32),
            pltpu.VMEM((slices, half, rows, share), jnp.float32),
            sems((2, 7)), sems((2, 7)),
            sems((slices + 1,)), sems((slices + 1,)), sems((slices + 1,)), sems((slices + 1,)),
            sems((slices + 1,)), sems((slices + 1,)), sems((5,)), sems((5,)), sems((3,)), sems((3,)),
            sems((8,)),
            sems((2, slices)), sems((2, slices)), sems((2, slices)), sems((2, slices)),
            sems((2, slices)), sems((2, slices)),
        ],
        compiler_params=pltpu.CompilerParams(
            collective_id=0, has_side_effects=True, vmem_limit_bytes=48 * 2**20),
        name="gather_factor",
    )(route, slot, pattern, diag, panel.reshape(blk, BS, share), contribution.reshape(blk, BS, share))


def split(value):
    high = value.astype(jnp.bfloat16)
    return high, (value - high.astype(jnp.float32)).astype(jnp.bfloat16)


def on_small(diag_block, panel, pattern, contribution, route, slot):
    rows, share = panel.shape[1:]
    blk = rows // BS
    factor, assembled, lower = factor_and_route(
        route.reshape(1, blk), slot.reshape(1, blk), pattern.reshape(1, blk),
        diag_block[0], panel[0], contribution[0])
    return (lower[None], factor.reshape(1, rows, share), assembled.reshape(1, rows // 2, share))


def from_root(value, axis, root):
    mine = lax.axis_index(axis) == root
    return lax.psum(jnp.where(mine, value, jnp.zeros_like(value)), axis)


def partner(value, axis, apart):
    mask = 2**apart
    pairs = [(source, source ^ mask) for source in range(lax.axis_size(axis))]
    return lax.ppermute(value, axis, pairs)


def on_large(diag_block, panel, pattern, contribution, route, slot):
    highest = lax.Precision.HIGHEST
    contract = (((1,), (1,)), ((), ()))
    whole = lax.all_gather(diag_block, ("row", "col"), axis=1, tiled=True)[0]
    width = whole.shape[0]
    lower = jnp.linalg.cholesky(whole)
    inverse = jax.scipy.linalg.solve_triangular(
        lower, jnp.eye(width, dtype=jnp.float32), lower=True
    )
    ncol = lax.axis_size("col")
    nrow = lax.axis_size("row")
    col_index = lax.axis_index("col")
    tile_mask = jnp.repeat(jnp.repeat(pattern[0], BS, axis=0), BS, axis=1).astype(jnp.float32)
    masked = panel[0] * tile_mask
    rows_dev = masked.shape[0]
    full_rows = lax.all_gather(masked, "col", axis=1, tiled=True)
    factor_rows = lax.dot_general(full_rows, inverse, contract, precision=highest)
    share = width // ncol
    own_cols = lax.dynamic_slice_in_dim(factor_rows, col_index * share, share, 1)
    cw_dev = contribution.shape[2]
    head_piece = lax.dynamic_slice_in_dim(factor_rows, col_index * cw_dev, cw_dev, 0)
    head_rows = from_root(head_piece, "row", 0)
    update = contribution[0] - lax.dot_general(factor_rows, head_rows, contract, precision=highest)
    blk = rows_dev // BS
    cap = max(2, blk // nrow)
    pblk = blk // 2
    blocks = update.reshape(blk, BS * cw_dev)
    target = route[0, :, 0]
    place = slot[0]
    order_ids = jnp.arange(blk, dtype=jnp.int32)
    earlier = (target[None, :] == target[:, None]) & (order_ids[None, :] < order_ids[:, None])
    rank = jnp.sum(earlier.astype(jnp.int32), axis=1)
    half = target // nrow
    target_row = target % nrow
    position = target_row * (2 * cap) + half * cap + rank
    slots_all = jnp.arange(nrow * 2 * cap, dtype=jnp.int32)
    onehot = (position[None, :] == slots_all[:, None]).astype(jnp.float32)
    packed = jnp.dot(onehot, blocks, precision=highest).reshape(nrow, 2, cap, BS * cw_dev)
    labels = jnp.dot(onehot, (place + 1).astype(jnp.float32), precision=highest).reshape(
        nrow, 2, cap
    )
    mine = lax.axis_index("cube") % 2
    got, got_labels = (
        lax.all_to_all(packed, "row", split_axis=0, concat_axis=0, tiled=True),
        lax.all_to_all(labels, "row", split_axis=0, concat_axis=0, tiled=True),
    )
    keep = lax.dynamic_index_in_dim(got, mine, 1, keepdims=False)
    keep_labels = lax.dynamic_index_in_dim(got_labels, mine, 1, keepdims=False)
    other = lax.dynamic_index_in_dim(got, 1 - mine, 1, keepdims=False)
    other_labels = lax.dynamic_index_in_dim(got_labels, 1 - mine, 1, keepdims=False)
    back, back_labels = partner((other, other_labels), "cube", 0)
    incoming = jnp.concatenate([keep, back], axis=0).reshape(-1, BS * cw_dev)
    tags = jnp.concatenate([keep_labels, back_labels], axis=0).reshape(-1)
    wanted = jnp.arange(1, pblk + 1, dtype=jnp.float32)
    select = (tags[None, :] == wanted[:, None]).astype(jnp.float32)
    assembled = jnp.dot(select, incoming, precision=highest).reshape(pblk * BS, cw_dev)
    rows_here = diag_block.shape[1]
    diag_rows = lax.dynamic_slice_in_dim(
        lower, lax.axis_index(("row", "col")) * rows_here, rows_here, 0
    )
    return (diag_rows[None], own_cols[None], assembled[None])


def solution(mesh):
    small = mesh.shape["row"] == 2 and mesh.shape["col"] == 4
    return jax.shard_map(
        on_small if small else on_large,
        mesh=mesh,
        in_specs=(
            P("cube", ("row", "col"), None),
            P("cube", "row", "col"),
            P("cube", "row", "col"),
            P("cube", "row", "col"),
            P("cube", "row", None),
            P("cube", "row"),
        ),
        out_specs=(
            P("cube", ("row", "col"), None),
            P("cube", "row", "col"),
            P("cube", "row", "col"),
        ),
        check_vma=False,
    )
```

time: 133 us -> 116 us (0.87)
  Pallas kernels: 120 us -> 111 us
  local copies, waits for them, and re-layouts: 8.2 us -> 3.99 us
  other arithmetic: 3.34 us -> 0 us
    pallas_call x1, Pallas kernels: 120 us -> 111 us  [factor_and_route(): pl.pallas_call(functools.partial(gather_kernel, rows), out_shape=(pltpu.V...]
    unnamed x5 -> x3, local copies, waits for them, and re-layouts: 7.51 us -> 3.99 us
    convert_element_type x3 -> x0, other arithmetic: 1.71 us -> none  [the longest x1 0.66 us: on_small(): mask = jnp.broadcast_to(pattern[0].astype(jnp.float32), (blk, share))]
where the time goes in v2:
time: 116 us
  Pallas kernels  111 us (96%)
  local copies, waits for them, and re-layouts  3.99 us (3%)
    pallas_call x1, Pallas kernels, factor_and_route(): pl.pallas_call(functools.partial(gather_kernel, rows), out_shape=(pltpu.V...  111 us
    unnamed x3, local copies, waits for them, and re-layouts  3.99 us

profile of v2, /device:TPU:0, one launch (start us, length us, event | category | flops | bytes accessed | tf_op | source)
XLA Modules:
  0.0 116.0 jit_solution(17263156177397888701)
XLA Ops:
  0.6 111.3 %gather_factor.1 = (f32[64,128,128]{2,1,0:T(8,128)S(1)}, f32[32,128,128]{2,1,0:T(8,128)S(1)}, f32[64,512]{1,0:T(8,128)S(1)}) custom-call(s32[1,64]{1,0:T(1,128)} %bitcast.14, s32[1,64]{1,0:T(1,128)} %slot_ref.1, s32[1,64]{1,0:T(1,128)} %bitcast.15, f32[64,512]{1,0:T(8,128)} %bitcast.13, f32[64,128,128]{2,1,0:T(8,128)} %bitcast.11, f32[64,128,128]{2,1,0:T(8,128)} %bitcast.12), custom_call_target="tpu_custom_call" | custom-call | tf_op jit(solution)/shard_map/gather_factor/pallas_call | solution.py:451
  112.0 0.7 copy.12
  112.6 2.0 %copy.13 = f32[1,8192,128]{2,1,0:T(8,128)} copy(f32[1,8192,128]{2,1,0:T(8,128)S(1)} %bitcast.8) | data formatting | bytes 8388608
  114.6 1.3 %copy.14 = f32[1,4096,128]{2,1,0:T(8,128)} copy(f32[1,4096,128]{2,1,0:T(8,128)S(1)} %bitcast.9) | data formatting | bytes 4194304

commit v3 on v2

--- a/solution.py
+++ b/solution.py
@@ -127,7 +127,7 @@
 
 def gather_kernel(rows, route_ref, slot_ref, pattern_ref, diag_ref, panel_ref, contribution_ref,
                   f_ref, out_ref, l_ref,
-                  own, g0, g1, g2, contrib, a_ref, inv_ref, s_ref, x_ref, r_ref, h_ref, hc_ref, v_ref,
+                  own, g0, g1, g2, contrib, a_ref, inv_ref, s_ref, x_ref, r_ref, hh_ref, h_ref, hc_ref, v_ref,
                   vh_ref, vl_ref, masks, head_masks, pats, head_pats, pattern, route, slot, table, names, upd, t_ref, ra, rb, ra2, rb2,
                   dsend, drecv, xsend, xrecv, fsend, frecv, psend, precv, hsend, hrecv,
                   msend, mrecv, isem, asend, arecv, bsend, brecv, lsend, lrecv):
@@ -176,17 +176,19 @@
             target[j] = jnp.broadcast_to(to_column(source[j, 0:1, 0:blocks]), target.shape[1:])
 
 
-    def piece_copy(k, n, rr, cc, device):
-        part = spot(rr, cc, k)
+    def even(rr, cc, k):
+        return spot(rr, cc, k)[0], pl.ds(pl.multiple_of((cc // 2 + 2 * k) * BS, BS), BS)
+
+    def piece_copy(k, n, part, device):
         return remote(a_ref.at[part], a_ref.at[part], dsend.at[k, n], drecv.at[k, n], device)
 
-    def own_copy(k, n, device):
-        part = spot(r, c, k)
+    def own_copy(k, n, part, device):
         return remote(diag_ref.at[:, part[1]], a_ref.at[part], dsend.at[k, n], drecv.at[k, n], device)
 
-    diag = [(own_copy(k, 0, to_x), own_copy(k, 1, to_row), piece_copy(k, 2, r, c2, to_row),
-             own_copy(k, 3, to_core), piece_copy(k, 4, r, c2, to_core), piece_copy(k, 5, y, c, to_core),
-             piece_copy(k, 6, y, c2, to_core)) for k in range(2)]
+    diag = [(own_copy(k, 0, even(r, c, k), to_x), own_copy(k, 1, spot(r, c, k), to_row),
+             piece_copy(k, 2, even(r, c2, k), to_row), own_copy(k, 3, spot(r, c, k), to_core),
+             piece_copy(k, 4, even(r, c2, k), to_core), piece_copy(k, 5, spot(y, c, k), to_core),
+             piece_copy(k, 6, even(y, c2, k), to_core)) for k in range(2)]
 
     def sliced(i):
         return (pl.ds(heads, blocks - heads), pl.ds(pl.multiple_of(i * rows, rows), rows))
@@ -202,6 +204,10 @@
     def beside(i, part):
         return remote(panel_ref.at[part], g0.at[part], psend.at[i], precv.at[i], to_core)
 
+    pair = pl.ds(2 * (c // 2), 2)
+    head = [remote(source.at[pair], hh_ref.at[k], hsend.at[k], hrecv.at[k], to_row)
+            for k, source in enumerate((panel_ref, g1))]
+    swap = [remote(hh_ref.at[k, 1 - c % 2], h_ref.at[k], hsend.at[2 + k], hrecv.at[2 + k], to_core) for k in range(2)]
     mask_x = remote(pats.at[0], pats.at[2], msend.at[0], mrecv.at[0], to_x)
     mask_core = remote(pats.at[0], pats.at[1], msend.at[1], mrecv.at[1], to_core)
     mask_on = remote(pats.at[2], pats.at[3], msend.at[2], mrecv.at[2], to_core)
@@ -210,6 +216,11 @@
         for n in (0, 1, 3):
             diag[k][n].start()
     mask_x.start()
+
+    @pl.when(r == 0)
+    def _():
+        head[0].start()
+
     across(slices, top).start()
     for i in range(slices):
         across(i, sliced(i)).start()
@@ -242,7 +253,17 @@
             for copy in copies:
                 copy.wait_send()
 
-    head = [remote(piece.at[c], h_ref.at[j], hsend.at[j], hrecv.at[j], to_row) for j, piece in enumerate(pieces)]
+        def mirror(i, j):
+            a_ref[i * BS:(i + 1) * BS, j * BS:(j + 1) * BS] = jnp.transpose(
+                a_ref[j * BS:(j + 1) * BS, i * BS:(i + 1) * BS])
+
+        for side in range(2):
+            @pl.when(c // 2 == side)
+            def _():
+                for i in range(1 - side, heads, 2):
+                    for j in range(i + 1, heads, 2):
+                        mirror(i, j)
+
     head_mask = remote(pats, head_pats, hsend.at[4], hrecv.at[4], to_row)
 
     def project(p):
@@ -258,6 +279,11 @@
         if p == 0:
             across(slices, top).wait_recv()
             onward(slices, top).start()
+
+            @pl.when(r == 0)
+            def _():
+                head[1].start()
+
             mask_x.wait_recv()
             mask_on.start()
             for i in range(slices):
@@ -275,21 +301,26 @@
 
             @pl.when(r == 0)
             def _():
-                for copy in head:
-                    copy.start()
                 head_mask.start()
                 for j, k in enumerate(order):
                     hc_ref[:, pl.ds(pl.multiple_of(k * BS, BS), BS)] = pieces[j][c] * masks[j, pl.ds(c, 1), :]
 
+            @pl.when(r == 1)
+            def _():
+                for k in range(2):
+                    head[k].wait_recv()
+                    swap[k].start()
+
         if p == 2:
             @pl.when(r == 1)
             def _():
-                for copy in head:
+                for copy in swap:
                     copy.wait_recv()
                 head_mask.wait_recv()
                 spread(head_pats, head_masks)
+                heads_in = (hh_ref[0, c % 2], h_ref[0], hh_ref[1, c % 2], h_ref[1])
                 for j, k in enumerate(order):
-                    hc_ref[:, pl.ds(pl.multiple_of(k * BS, BS), BS)] = h_ref[j] * head_masks[j, pl.ds(c, 1), :]
+                    hc_ref[:, pl.ds(pl.multiple_of(k * BS, BS), BS)] = heads_in[j] * head_masks[j, pl.ds(c, 1), :]
 
             for q in range(3):
                 project(q)
@@ -337,14 +368,15 @@
 
         lax.fori_loop(0, blocks // group, tile, 0)
 
-        def fill(q, carry):
+    def fill(i, start):
+        def body(q, carry):
             for b in range(16):
-                k = q * 16 + b
+                k = start + q * 16 + b
                 name = names[1, k]
                 t_ref[i, k] = upd[jnp.clip(name - 1, 0, blocks - 1)] * jnp.where(name > 0, 1.0, 0.0)
             return carry
 
-        lax.fori_loop(0, 4 * slots // 16, fill, 0)
+        lax.fori_loop(0, half // 16, body, 0)
 
     def quarter(g, low):
         return pl.ds(g * slots + (0 if low else half), half)
@@ -400,9 +432,17 @@
             onward(i, sliced(i)).wait_recv()
             compute(i)
             over_a, over_b, _ = hops(i)
-            for k in range(2):
-                over_a[k].start()
-                over_b[k].start()
+            here, there, above = (m * 2 + y) * slots, ((1 - m) * 2 + y) * slots, ((1 - m) * 2 + r) * slots
+            fill(i, there)
+            over_a[0].start()
+            fill(i, there + half)
+            over_b[0].start()
+            fill(i, here)
+            over_a[1].start()
+            fill(i, above + half)
+            over_b[1].start()
+            for start in (above, here + half, (m * 2 + r) * slots, (m * 2 + r) * slots + half):
+                fill(i, start)
 
         @pl.when((i > 0) & (i <= slices) & (i != slices - 1))
         def _():
@@ -434,6 +474,11 @@
         for copy in head:
             copy.wait_send()
         head_mask.wait_send()
+
+    @pl.when(r == 1)
+    def _():
+        for copy in swap:
+            copy.wait_send()
 
 
 def factor_and_route(route, slot, pattern, diag, panel, contribution):
@@ -461,7 +506,8 @@
             whole, whole, whole, whole, whole,
             square, square, block, block,
             pltpu.VMEM((BS, width), jnp.float32),
-            pltpu.VMEM((4, BS, BS), jnp.float32),
+            pltpu.VMEM((2, 2, BS, BS), jnp.float32),
+            pltpu.VMEM((2, BS, BS), jnp.float32),
             pltpu.VMEM((BS, width), jnp.float32),
             pltpu.VMEM((width, BS), jnp.float32),
             pltpu.VMEM((width, 2 * BS), jnp.bfloat16),
@@ -499,12 +545,38 @@
     return high, (value - high.astype(jnp.float32)).astype(jnp.bfloat16)
 
 
+def store_kernel(parts, f_ref, out_ref, l_ref, f_hbm, out_hbm, l_hbm, sem):
+    copies = [pltpu.make_async_copy(l_ref, l_hbm, sem.at[0])]
+    for source, target in ((f_ref, f_hbm), (out_ref, out_hbm)):
+        n = source.shape[0] // parts
+        for k in range(parts):
+            part = pl.ds(k * n, n)
+            copies.append(pltpu.make_async_copy(source.at[part], target.at[part], sem.at[len(copies)]))
+    for copy in copies:
+        copy.start()
+    for copy in copies:
+        copy.wait()
+
+
+def store(values):
+    parts = 1
+    return pl.pallas_call(
+        functools.partial(store_kernel, parts),
+        out_shape=[jax.ShapeDtypeStruct(value.shape, value.dtype) for value in values],
+        in_specs=[ANY] * 3,
+        out_specs=[ANY] * 3,
+        scratch_shapes=[pltpu.SemaphoreType.DMA((2 * parts + 1,))],
+        compiler_params=pltpu.CompilerParams(vmem_limit_bytes=2**20),
+        name="store",
+    )(*values)
+
+
 def on_small(diag_block, panel, pattern, contribution, route, slot):
     rows, share = panel.shape[1:]
     blk = rows // BS
-    factor, assembled, lower = factor_and_route(
+    factor, assembled, lower = store(factor_and_route(
         route.reshape(1, blk), slot.reshape(1, blk), pattern.reshape(1, blk),
-        diag_block[0], panel[0], contribution[0])
+        diag_block[0], panel[0], contribution[0]))
     return (lower[None], factor.reshape(1, rows, share), assembled.reshape(1, rows // 2, share))
 
 

time: 116 us -> 113 us (0.974)
  local copies, waits for them, and re-layouts: 3.99 us -> 0 us
    unnamed x3 -> x0, local copies, waits for them, and re-layouts: 3.99 us -> none
    pallas_call x0 -> x1, Pallas kernels: none -> 2.77 us  [store(): pl.pallas_call(functools.partial(store_kernel, parts), out_shape=[jax.Sha...]
    pallas_call x1, Pallas kernels: 111 us -> 109 us  [factor_and_route(): pl.pallas_call(functools.partial(gather_kernel, rows), out_shape=(pltpu.V...]
where the time goes in v3:
time: 113 us
  Pallas kernels  112 us (99%)
    pallas_call x1, Pallas kernels, factor_and_route(): pl.pallas_call(functools.partial(gather_kernel, rows), out_shape=(pltpu.V...  109 us
    pallas_call x1, Pallas kernels, store(): pl.pallas_call(functools.partial(store_kernel, parts), out_shape=[jax.Sha...  2.77 us

profile of v3, /device:TPU:0, one launch (start us, length us, event | category | flops | bytes accessed | tf_op | source)
XLA Modules:
  0.0 112.9 jit_solution(14044614358497157600)
XLA Ops:
  0.6 109.4 %gather_factor.1 = (f32[64,128,128]{2,1,0:T(8,128)S(1)}, f32[32,128,128]{2,1,0:T(8,128)S(1)}, f32[64,512]{1,0:T(8,128)S(1)}) custom-call(s32[1,64]{1,0:T(1,128)} %bitcast.11, s32[1,64]{1,0:T(1,128)} %slot_ref.1, s32[1,64]{1,0:T(1,128)} %bitcast.12, f32[64,512]{1,0:T(8,128)} %bitcast.10, f32[64,128,128]{2,1,0:T(8,128)} %bitcast.8, f32[64,128,128]{2,1,0:T(8,128)} %bitcast.9), custom_call_target="tpu_custom_call" | custom-call | tf_op jit(solution)/shard_map/gather_factor/pallas_call | solution.py:496
  110.0 2.8 %store.1 = (f32[64,128,128]{2,1,0:T(8,128)}, f32[32,128,128]{2,1,0:T(8,128)}, f32[64,512]{1,0:T(8,128)}) custom-call(f32[64,128,128]{2,1,0:T(8,128)S(1)} %get-tuple-element.9.f_ref, f32[32,128,128]{2,1,0:T(8,128)S(1)} %get-tuple-element.10.out_ref, f32[64,512]{1,0:T(8,128)S(1)} %get-tuple-element.11.l_ref), custom_call_target="tpu_custom_call" | custom-call | tf_op jit(solution)/shard_map/store/pallas_call | solution.py:563

commit v4 on v3

--- a/solution.py
+++ b/solution.py
@@ -128,7 +128,7 @@
 def gather_kernel(rows, route_ref, slot_ref, pattern_ref, diag_ref, panel_ref, contribution_ref,
                   f_ref, out_ref, l_ref,
                   own, g0, g1, g2, contrib, a_ref, inv_ref, s_ref, x_ref, r_ref, hh_ref, h_ref, hc_ref, v_ref,
-                  vh_ref, vl_ref, masks, head_masks, pats, head_pats, pattern, route, slot, table, names, upd, t_ref, ra, rb, ra2, rb2,
+                  vh_ref, vl_ref, masks, head_masks, pats, head_pats, pattern, route, slot, table, names, acc, upd, t_ref, ra, rb, ra2, rb2,
                   dsend, drecv, xsend, xrecv, fsend, frecv, psend, precv, hsend, hrecv,
                   msend, mrecv, isem, asend, arecv, bsend, brecv, lsend, lrecv):
     z = lax.axis_index("cube")
@@ -226,8 +226,6 @@
         across(i, sliced(i)).start()
     mask_core.start()
     beside(slices, top).start()
-    load_own.start()
-    load_contrib.start()
     for k in range(2):
         diag[k][0].wait_recv()
         diag[k][2].start()
@@ -241,6 +239,7 @@
                 diag[k][n].wait_recv()
     for copy in load_diag:
         copy.wait()
+    load_own.start()
 
     def middle():
         diag[1][2].wait_recv()
@@ -292,7 +291,7 @@
             load_table.start()
         if p == 1:
             load_own.wait()
-            load_contrib.wait()
+            load_contrib.start()
             beside(slices, top).wait_recv()
             onward(slices, top).wait_recv()
             mask_core.wait_recv()
@@ -344,29 +343,33 @@
             l_ref[:, k * BS:(k + 1) * BS] = s_ref[pl.ds(pl.multiple_of((c % 2) * ndiag, ndiag), ndiag), :]
 
     load_table.wait()
-    group = min(blocks, 512 // rows)
-
-    def compute(i):
+    load_contrib.wait()
+    def product(i, first):
         part = pl.ds(pl.multiple_of(i * rows, rows), rows)
-
-        def tile(q, carry):
-            lines = []
-            for b in range(group):
-                at = q * group + b
-                lines.append(jnp.concatenate(
-                    [piece[at, part] * masks[j, pl.ds(at, 1), :] for j, piece in enumerate(pieces)], axis=1))
-            high, low = split(jnp.concatenate(lines, axis=0))
-            dot = functools.partial(jnp.dot, preferred_element_type=jnp.float32)
-            out = dot(high, vh_ref[...]) + (dot(high, vl_ref[...]) + dot(low, vh_ref[...]))
-            for b in range(group):
-                at = q * group + b
-                f_ref[at, part] = out[b * rows:(b + 1) * rows, :BS]
-                update = contrib[at, part] - out[b * rows:(b + 1) * rows, BS:]
-                name = names[0, at]
-                upd[at] = update + jnp.where(name > 0, 1.0, 0.0) * upd[jnp.clip(name - 1, 0, blocks - 1)]
-            return carry
-
-        lax.fori_loop(0, blocks // group, tile, 0)
+        lines = []
+        for at in range(blocks):
+            lines.append(jnp.concatenate(
+                [pieces[j][at, part] * masks[j, pl.ds(at, 1), :] for j in (first, first + 1)], axis=1))
+        high, low = split(jnp.concatenate(lines, axis=0))
+        dot = functools.partial(jnp.dot, preferred_element_type=jnp.float32)
+        side = slice(first * BS, (first + 2) * BS)
+        return dot(high, vh_ref[side]) + (dot(high, vl_ref[side]) + dot(low, vh_ref[side]))
+
+    def early(i):
+        part = pl.ds(pl.multiple_of(i * rows, rows), rows)
+        out = product(i, 0)
+        for at in range(blocks):
+            f_ref[at, part] = out[at * rows:(at + 1) * rows, :BS]
+            acc[at] = contrib[at, part] - out[at * rows:(at + 1) * rows, BS:]
+
+    def late(i):
+        part = pl.ds(pl.multiple_of(i * rows, rows), rows)
+        out = product(i, 2)
+        for at in range(blocks):
+            f_ref[at, part] = f_ref[at, part] + out[at * rows:(at + 1) * rows, :BS]
+            update = acc[at] - out[at * rows:(at + 1) * rows, BS:]
+            name = names[0, at]
+            upd[at] = update + jnp.where(name > 0, 1.0, 0.0) * upd[jnp.clip(name - 1, 0, blocks - 1)]
 
     def fill(i, start):
         def body(q, carry):
@@ -419,6 +422,8 @@
 
         @pl.when(i < slices)
         def _():
+            beside(i, sliced(i)).wait_recv()
+            early(i)
             across(i, sliced(i)).wait_recv()
             onward(i, sliced(i)).start()
 
@@ -428,9 +433,8 @@
 
         @pl.when(i < slices)
         def _():
-            beside(i, sliced(i)).wait_recv()
             onward(i, sliced(i)).wait_recv()
-            compute(i)
+            late(i)
             over_a, over_b, _ = hops(i)
             here, there, above = (m * 2 + y) * slots, ((1 - m) * 2 + y) * slots, ((1 - m) * 2 + r) * slots
             fill(i, there)
@@ -521,6 +525,7 @@
             pltpu.VMEM((1, blk), jnp.int32),
             pltpu.VMEM((8, BS), jnp.int32),
             pltpu.SMEM((8, BS), jnp.int32),
+            pltpu.VMEM((blk, rows, share), jnp.float32),
             pltpu.VMEM((blk, rows, share), jnp.float32),
             pltpu.VMEM((slices, 4 * pblk, rows, share), jnp.float32),
             pltpu.VMEM((2, slices, half, rows, share), jnp.float32),

time: 113 us -> 113 us (level)
  no operation moved by 1% of the time
where the time goes in v4:
time: 113 us
  Pallas kernels  112 us (99%)
    pallas_call x1, Pallas kernels, factor_and_route(): pl.pallas_call(functools.partial(gather_kernel, rows), out_shape=(pltpu.V...  109 us
    pallas_call x1, Pallas kernels, store(): pl.pallas_call(functools.partial(store_kernel, parts), out_shape=[jax.Sha...  2.77 us

profile of v4, /device:TPU:0, one launch (start us, length us, event | category | flops | bytes accessed | tf_op | source)
XLA Modules:
  0.0 113.0 jit_solution(12822656142036448911)
XLA Ops:
  0.6 109.4 %gather_factor.1 = (f32[64,128,128]{2,1,0:T(8,128)S(1)}, f32[32,128,128]{2,1,0:T(8,128)S(1)}, f32[64,512]{1,0:T(8,128)S(1)}) custom-call(s32[1,64]{1,0:T(1,128)} %bitcast.11, s32[1,64]{1,0:T(1,128)} %slot_ref.1, s32[1,64]{1,0:T(1,128)} %bitcast.12, f32[64,512]{1,0:T(8,128)} %bitcast.10, f32[64,128,128]{2,1,0:T(8,128)} %bitcast.8, f32[64,128,128]{2,1,0:T(8,128)} %bitcast.9), custom_call_target="tpu_custom_call" | custom-call | tf_op jit(solution)/shard_map/gather_factor/pallas_call | solution.py:500
  110.0 2.8 %store.1 = (f32[64,128,128]{2,1,0:T(8,128)}, f32[32,128,128]{2,1,0:T(8,128)}, f32[64,512]{1,0:T(8,128)}) custom-call(f32[64,128,128]{2,1,0:T(8,128)S(1)} %get-tuple-element.9.f_ref, f32[32,128,128]{2,1,0:T(8,128)S(1)} %get-tuple-element.10.out_ref, f32[64,512]{1,0:T(8,128)S(1)} %get-tuple-element.11.l_ref), custom_call_target="tpu_custom_call" | custom-call | tf_op jit(solution)/shard_map/store/pallas_call | solution.py:568

commit v5 on v4

--- a/solution.py
+++ b/solution.py
@@ -160,15 +160,12 @@
     load_table = pltpu.make_async_copy(table, names, isem.at[4])
     load_small = [pltpu.make_async_copy(source, target, isem.at[5 + k]) for k, (source, target) in enumerate(
         ((pattern_ref, pattern), (route_ref, route), (slot_ref, slot)))]
-    for copy in load_small + load_diag:
-        copy.start()
-    pats[...] = jnp.zeros_like(pats)
     barrier = pltpu.get_barrier_semaphore()
     for device in (to_x, to_core, to_row, to_cube):
         pl.semaphore_signal(barrier, inc=1, device_id=device, device_id_type=MESH)
-    for copy in load_small:
-        copy.wait()
-    pats[0, 0:1, 0:blocks] = pattern[...].astype(jnp.float32)
+    for copy in load_small + load_diag:
+        copy.start()
+    pats[0] = jnp.zeros(pats.shape[1:], jnp.float32)
     pl.semaphore_wait(barrier, 4)
 
     def spread(source, target):
@@ -215,13 +212,16 @@
     for k in range(2):
         for n in (0, 1, 3):
             diag[k][n].start()
-    mask_x.start()
 
     @pl.when(r == 0)
     def _():
         head[0].start()
 
     across(slices, top).start()
+    for copy in load_small:
+        copy.wait()
+    pats[0, 0:1, 0:blocks] = pattern[...].astype(jnp.float32)
+    mask_x.start()
     for i in range(slices):
         across(i, sliced(i)).start()
     mask_core.start()

time: 113 us -> 113 us (level)
  no operation moved by 1% of the time
where the time goes in v5:
time: 113 us
  Pallas kernels  112 us (99%)
    pallas_call x1, Pallas kernels, factor_and_route(): pl.pallas_call(functools.partial(gather_kernel, rows), out_shape=(pltpu.V...  109 us
    pallas_call x1, Pallas kernels, store(): pl.pallas_call(functools.partial(store_kernel, parts), out_shape=[jax.Sha...  2.77 us

profile of v5, /device:TPU:0, one launch (start us, length us, event | category | flops | bytes accessed | tf_op | source)
XLA Modules:
  0.0 112.6 jit_solution(2897132526975846269)
XLA Ops:
  0.6 109.0 %gather_factor.1 = (f32[64,128,128]{2,1,0:T(8,128)S(1)}, f32[32,128,128]{2,1,0:T(8,128)S(1)}, f32[64,512]{1,0:T(8,128)S(1)}) custom-call(s32[1,64]{1,0:T(1,128)} %bitcast.11, s32[1,64]{1,0:T(1,128)} %slot_ref.1, s32[1,64]{1,0:T(1,128)} %bitcast.12, f32[64,512]{1,0:T(8,128)} %bitcast.10, f32[64,128,128]{2,1,0:T(8,128)} %bitcast.8, f32[64,128,128]{2,1,0:T(8,128)} %bitcast.9), custom_call_target="tpu_custom_call" | custom-call | tf_op jit(solution)/shard_map/gather_factor/pallas_call | solution.py:500
  109.7 2.8 %store.1 = (f32[64,128,128]{2,1,0:T(8,128)}, f32[32,128,128]{2,1,0:T(8,128)}, f32[64,512]{1,0:T(8,128)}) custom-call(f32[64,128,128]{2,1,0:T(8,128)S(1)} %get-tuple-element.9.f_ref, f32[32,128,128]{2,1,0:T(8,128)S(1)} %get-tuple-element.10.out_ref, f32[64,512]{1,0:T(8,128)S(1)} %get-tuple-element.11.l_ref), custom_call_target="tpu_custom_call" | custom-call | tf_op jit(solution)/shard_map/store/pallas_call | solution.py:568

commit v6 on v5

--- a/solution.py
+++ b/solution.py
@@ -415,10 +415,26 @@
 
     upd[...] = jnp.zeros_like(upd)
 
+    def settle():
+        for copy in (across(slices, top), onward(slices, top), beside(slices, top), mask_x, mask_core, mask_on):
+            copy.wait_send()
+
+        @pl.when(r == 0)
+        def _():
+            for copy in head:
+                copy.wait_send()
+            head_mask.wait_send()
+
+        @pl.when(r == 1)
+        def _():
+            for copy in swap:
+                copy.wait_send()
+
     def step(i, carry):
         @pl.when(i == 3)
         def _():
             lower_rows()
+            settle()
 
         @pl.when(i < slices)
         def _():
@@ -456,9 +472,9 @@
         def _():
             finish(i - 3)
 
-        @pl.when(i > 3)
-        def _():
-            drain(i - 4)
+        @pl.when(i > 2)
+        def _():
+            drain(i - 3)
         return carry
 
     def drain(i):
@@ -467,22 +483,6 @@
             copy.wait_send()
 
     lax.fori_loop(0, slices + 3, step, 0)
-
-    for i in (slices - 1,):
-        drain(i)
-    for copy in (across(slices, top), onward(slices, top), beside(slices, top), mask_x, mask_core, mask_on):
-        copy.wait_send()
-
-    @pl.when(r == 0)
-    def _():
-        for copy in head:
-            copy.wait_send()
-        head_mask.wait_send()
-
-    @pl.when(r == 1)
-    def _():
-        for copy in swap:
-            copy.wait_send()
 
 
 def factor_and_route(route, slot, pattern, diag, panel, contribution):

time: 113 us -> 113 us (level)
  no operation moved by 1% of the time
where the time goes in v6:
time: 113 us
  Pallas kernels  112 us (99%)
    pallas_call x1, Pallas kernels, factor_and_route(): pl.pallas_call(functools.partial(gather_kernel, rows), out_shape=(pltpu.V...  109 us
    pallas_call x1, Pallas kernels, store(): pl.pallas_call(functools.partial(store_kernel, parts), out_shape=[jax.Sha...  2.77 us

profile of v6, /device:TPU:0, one launch (start us, length us, event | category | flops | bytes accessed | tf_op | source)
XLA Modules:
  0.0 112.6 jit_solution(3101633071852585915)
XLA Ops:
  0.6 109.0 %gather_factor.1 = (f32[64,128,128]{2,1,0:T(8,128)S(1)}, f32[32,128,128]{2,1,0:T(8,128)S(1)}, f32[64,512]{1,0:T(8,128)S(1)}) custom-call(s32[1,64]{1,0:T(1,128)} %bitcast.11, s32[1,64]{1,0:T(1,128)} %slot_ref.1, s32[1,64]{1,0:T(1,128)} %bitcast.12, f32[64,512]{1,0:T(8,128)} %bitcast.10, f32[64,128,128]{2,1,0:T(8,128)} %bitcast.8, f32[64,128,128]{2,1,0:T(8,128)} %bitcast.9), custom_call_target="tpu_custom_call" | custom-call | tf_op jit(solution)/shard_map/gather_factor/pallas_call | solution.py:500
  109.6 2.8 %store.1 = (f32[64,128,128]{2,1,0:T(8,128)}, f32[32,128,128]{2,1,0:T(8,128)}, f32[64,512]{1,0:T(8,128)}) custom-call(f32[64,128,128]{2,1,0:T(8,128)S(1)} %get-tuple-element.9.f_ref, f32[32,128,128]{2,1,0:T(8,128)S(1)} %get-tuple-element.10.out_ref, f32[64,512]{1,0:T(8,128)S(1)} %get-tuple-element.11.l_ref), custom_call_target="tpu_custom_call" | custom-call | tf_op jit(solution)/shard_map/store/pallas_call | solution.py:568
